TPU v7x, 32 devices: a whole 2x2x4 slice. The times are simulated.
32 devices in a mesh: replica: 2 (over y), fsdp: 8 (over z, core), seq: 2 (over x).
Axes of the slice: x: 2, y: 2, z: 4, core: 2. Of those that a mesh axis runs over, the one named last changes fastest.
Arguments:
- series_in: bfloat16 [16, 512, 1280], P(('replica', 'fsdp'), 'seq'), may hold values from -6 to 6
- cotangent: bfloat16 [16, 512, 1280], P(('replica', 'fsdp'), 'seq'), may hold values from -6 to 6
- qkv_weight: bfloat16 [2, 1280, 3840], P(None, 'fsdp'), may hold values from -0.15625 to 0.15625
- out_weight: bfloat16 [2, 1280, 1280], P(None, 'fsdp'), may hold values from -0.625 to 0.625
- up_weight: bfloat16 [2, 1280, 1280], P(None, 'fsdp'), may hold values from -0.15625 to 0.15625
- down_weight: bfloat16 [2, 1280, 1280], P(None, 'fsdp'), may hold values from -0.15625 to 0.15625
- norm_gains: bfloat16 [2, 2, 1280], P(None, None, 'fsdp'), may hold values from 0.25 to 1.75
- up_bias: bfloat16 [2, 1280], P(None, 'fsdp'), may hold values from -3 to 3
- down_bias: bfloat16 [2, 1280], P(None, 'fsdp'), may hold values from -2 to 2
- query_scale: bfloat16 [2, 80], P(None, 'fsdp'), may hold values from -1 to 1
- pad_length: int32 [16], P(('replica', 'fsdp')), may hold values from 0 to 128, as said below
- span_starts: int32 [16, 4], P(('replica', 'fsdp')), may hold values from 0 to 480, as said below
- span_count: int32 [16], P(('replica', 'fsdp')), may hold values from 1 to 4, as said below
Outputs:
- series_out: bfloat16 [16, 512, 1280], P(('replica', 'fsdp'), 'seq')
- input_grad: bfloat16 [16, 512, 1280], P(('replica', 'fsdp'), 'seq')
- grad_qkv: float32 [2, 1280, 3840], P(None, 'fsdp')
- grad_out: float32 [2, 1280, 1280], P(None, 'fsdp')
- grad_up: float32 [2, 1280, 1280], P(None, 'fsdp')
- grad_down: float32 [2, 1280, 1280], P(None, 'fsdp')
- grad_gains: float32 [2, 2, 1280], P(None, None, 'fsdp')
- grad_up_bias: float32 [2, 1280], P(None, 'fsdp')
- grad_down_bias: float32 [2, 1280], P(None, 'fsdp')
- grad_query_scale: float32 [2, 80], P(None, 'fsdp')
Inputs may be any that keep to these rules, and one draw needn't show every extreme that they name: `pad_length`: one series in every draw has exactly 128 padded positions. `span_starts`: slot 0 of every series starts within 31 positions before 256, so it holds positions 255 and 256; spans may intersect. Slot k of series b is used when k < span_count[b].
All inputs are finite; a program needn't handle non-finite values.
Results may differ from a plain program's by a relative error of at most 0.025.
Values may be sent and summed in bfloat16 or wider, within the bound.
A program may use at most 256 MiB of HBM per device.

v0:
```python
import math

import jax
import jax.numpy as jnp
from jax import lax
from jax.sharding import PartitionSpec as P

HEADS = 16
HEAD = 80
SPAN = 32


EPSILON = 1e-06
SOFT_ONE = 1.442695041
NEG_FILL = -1e30


def visible(pad_length, span_starts, span_count, offset, local_length, total_length):
    query_pos = offset + jnp.arange(local_length, dtype=jnp.int32)
    key_pos = jnp.arange(total_length, dtype=jnp.int32)
    shared = jnp.zeros((span_starts.shape[0], local_length, total_length), dtype=bool)
    for slot_index in range(span_starts.shape[1]):
        slot_start = span_starts[:, slot_index]
        slot_used = slot_index < span_count
        query_in = (
            slot_used[:, None]
            & (query_pos[None, :] >= slot_start[:, None])
            & (query_pos[None, :] < slot_start[:, None] + SPAN)
        )
        key_in = (key_pos[None, :] >= slot_start[:, None]) & (
            key_pos[None, :] < slot_start[:, None] + SPAN
        )
        shared = shared | query_in[:, :, None] & key_in[:, None, :]
    causal = key_pos[None, :] <= query_pos[:, None]
    allowed = (key_pos[None, None, :] >= pad_length[:, None, None]) & (causal[None] | shared)
    return allowed | (key_pos[None, None, :] == query_pos[None, :, None])


def norm_rows(values, scale_gain):
    inverse = lax.rsqrt(jnp.mean(values * values, axis=-1, keepdims=True) + EPSILON)
    return (values * inverse * scale_gain, inverse)


def norm_back(values, inverse, scale_gain, upstream):
    scaled = upstream * scale_gain
    inner_term = jnp.mean(values * scaled, axis=-1, keepdims=True)
    result = inverse * scaled - values * (inverse * inverse * inverse) * inner_term
    return (result, jnp.sum(upstream * values * inverse, axis=0))


def query_factor(query_scale):
    return jax.nn.softplus(query_scale.astype(jnp.float32)) * (SOFT_ONE / math.sqrt(HEAD))


def forward_layer(current, weights, allowed, series_count, local_length, total_length):
    qkv_weight, out_weight, up_weight, down_weight, norm_gains, up_bias, down_bias, query_scale = (
        weights
    )
    token_count, model_width = current.shape
    normed, inverse_one = norm_rows(current, norm_gains[0].astype(jnp.float32))
    normed_low = normed.astype(jnp.bfloat16).reshape(series_count, local_length, model_width)
    projected = jnp.einsum(
        "bld,dc->bcl", normed_low, qkv_weight, preferred_element_type=jnp.float32
    )
    query_raw = projected[:, :model_width]
    factor = query_factor(query_scale)
    query_low = (
        query_raw.reshape(series_count, HEADS, HEAD, local_length) * factor[None, None, :, None]
    ).astype(jnp.bfloat16)
    pair_low = projected[:, model_width:].astype(jnp.bfloat16)
    pair_all = lax.all_gather(pair_low, "seq", axis=2, tiled=True)
    key_all = pair_all[:, :model_width].reshape(series_count, HEADS, HEAD, total_length)
    value_all = pair_all[:, model_width:].reshape(series_count, HEADS, HEAD, total_length)
    scores = jnp.einsum("bheq,bhek->bhqk", query_low, key_all, preferred_element_type=jnp.float32)
    scores = jnp.where(allowed[:, None], scores, NEG_FILL)
    top_score = jnp.max(scores, axis=-1, keepdims=True)
    exp_scores = jnp.exp(scores - top_score)
    exp_total = jnp.sum(exp_scores, axis=-1, keepdims=True)
    probs_low = (exp_scores / exp_total).astype(jnp.bfloat16)
    log_total = top_score + jnp.log(exp_total)
    attended = jnp.einsum(
        "bhqk,bhek->bheq", probs_low, value_all, preferred_element_type=jnp.float32
    )
    attended_low = attended.astype(jnp.bfloat16).reshape(series_count, model_width, local_length)
    attn_out = jnp.einsum(
        "bdl,de->ble", attended_low, out_weight, preferred_element_type=jnp.float32
    )
    after_attn = current + attn_out.reshape(token_count, model_width)
    normed_two, inverse_two = norm_rows(after_attn, norm_gains[1].astype(jnp.float32))
    mixed_low = normed_two.astype(jnp.bfloat16)
    hidden_pre = jnp.dot(mixed_low, up_weight, preferred_element_type=jnp.float32) + up_bias.astype(
        jnp.float32
    )
    hidden_low = jax.nn.silu(hidden_pre).astype(jnp.bfloat16)
    result = after_attn + (
        jnp.dot(hidden_low, down_weight, preferred_element_type=jnp.float32)
        + down_bias.astype(jnp.float32)
    )
    stored = (
        current,
        inverse_one,
        normed_low,
        query_raw,
        query_low,
        key_all,
        value_all,
        log_total,
        attended_low,
        after_attn,
        inverse_two,
        mixed_low,
        hidden_pre,
        hidden_low,
    )
    return (result, stored)


def backward_layer(upstream, weights, stored, allowed, series_count, local_length, total_length):
    qkv_weight, out_weight, up_weight, down_weight, norm_gains, up_bias, down_bias, query_scale = (
        weights
    )
    (
        current,
        inverse_one,
        normed_low,
        query_raw,
        query_low,
        key_all,
        value_all,
        log_total,
        attended_low,
        after_attn,
        inverse_two,
        mixed_low,
        hidden_pre,
        hidden_low,
    ) = stored
    token_count, model_width = current.shape
    down_low = upstream.astype(jnp.bfloat16)
    grad_down_bias = jnp.sum(down_low, axis=0, dtype=jnp.float32)
    grad_down = jnp.einsum("tf,td->fd", hidden_low, down_low, preferred_element_type=jnp.float32)
    hidden_grad = jnp.einsum("td,fd->tf", down_low, down_weight, preferred_element_type=jnp.float32)
    sigmoid_pre = jax.nn.sigmoid(hidden_pre)
    pre_low = (hidden_grad * sigmoid_pre * (1.0 + hidden_pre * (1.0 - sigmoid_pre))).astype(
        jnp.bfloat16
    )
    grad_up_bias = jnp.sum(pre_low, axis=0, dtype=jnp.float32)
    grad_up = jnp.einsum("td,tf->df", mixed_low, pre_low, preferred_element_type=jnp.float32)
    mixed_grad = jnp.einsum("tf,df->td", pre_low, up_weight, preferred_element_type=jnp.float32)
    norm_grad_two, gain_grad_two = norm_back(
        after_attn, inverse_two, norm_gains[1].astype(jnp.float32), mixed_grad
    )
    attn_grad = upstream + norm_grad_two
    branch_low = attn_grad.astype(jnp.bfloat16).reshape(series_count, local_length, model_width)
    grad_out = jnp.einsum(
        "bdl,ble->de", attended_low, branch_low, preferred_element_type=jnp.float32
    )
    output_low = (
        jnp.einsum("ble,de->bdl", branch_low, out_weight, preferred_element_type=jnp.float32)
        .astype(jnp.bfloat16)
        .reshape(series_count, HEADS, HEAD, local_length)
    )
    scores = jnp.einsum("bheq,bhek->bhqk", query_low, key_all, preferred_element_type=jnp.float32)
    scores = jnp.where(allowed[:, None], scores, NEG_FILL)
    attn_probs = jnp.exp(scores - log_total)
    prob_grad = jnp.einsum(
        "bheq,bhek->bhqk", output_low, value_all, preferred_element_type=jnp.float32
    )
    row_inner = jnp.sum(attn_probs * prob_grad, axis=-1, keepdims=True)
    score_low = (attn_probs * (prob_grad - row_inner)).astype(jnp.bfloat16)
    value_grad = jnp.einsum(
        "bhqk,bheq->bhek",
        attn_probs.astype(jnp.bfloat16),
        output_low,
        preferred_element_type=jnp.float32,
    )
    key_grad = jnp.einsum(
        "bhqk,bheq->bhek", score_low, query_low, preferred_element_type=jnp.float32
    )
    query_grad = jnp.einsum(
        "bhqk,bhek->bheq", score_low, key_all, preferred_element_type=jnp.float32
    )
    key_local, value_local = (
        lax.psum_scatter(
            key_grad.reshape(series_count, model_width, total_length),
            "seq",
            scatter_dimension=2,
            tiled=True,
        ),
        lax.psum_scatter(
            value_grad.reshape(series_count, model_width, total_length),
            "seq",
            scatter_dimension=2,
            tiled=True,
        ),
    )
    factor = query_factor(query_scale)
    factor_grad = jnp.sum(
        query_grad * query_raw.reshape(series_count, HEADS, HEAD, local_length), axis=(0, 1, 3)
    )
    grad_scale = (
        factor_grad * jax.nn.sigmoid(query_scale.astype(jnp.float32)) * (SOFT_ONE / math.sqrt(HEAD))
    )
    raw_low = (
        (query_grad * factor[None, None, :, None])
        .astype(jnp.bfloat16)
        .reshape(series_count, model_width, local_length)
    )
    projected_grad = jnp.concatenate(
        [raw_low, key_local.astype(jnp.bfloat16), value_local.astype(jnp.bfloat16)], axis=1
    )
    grad_qkv = jnp.einsum(
        "bld,bcl->dc", normed_low, projected_grad, preferred_element_type=jnp.float32
    )
    normed_grad = jnp.einsum(
        "bcl,dc->bld", projected_grad, qkv_weight, preferred_element_type=jnp.float32
    ).reshape(token_count, model_width)
    norm_grad_one, gain_grad_one = norm_back(
        current, inverse_one, norm_gains[0].astype(jnp.float32), normed_grad
    )
    result = attn_grad + norm_grad_one
    layer_grads = (
        grad_qkv,
        grad_out,
        grad_up,
        grad_down,
        jnp.stack([gain_grad_one, gain_grad_two]),
        grad_up_bias,
        grad_down_bias,
        grad_scale,
    )
    return (result, layer_grads)


def shards(
    series_in,
    cotangent,
    qkv_weight,
    out_weight,
    up_weight,
    down_weight,
    norm_gains,
    up_bias,
    down_bias,
    query_scale,
    pad_length,
    span_starts,
    span_count,
):
    series_count, local_length, model_width = series_in.shape
    seq_count = lax.axis_size("seq")
    total_length = local_length * seq_count
    offset = lax.axis_index("seq") * local_length
    allowed = visible(pad_length, span_starts, span_count, offset, local_length, total_length)
    layer_count = qkv_weight.shape[0]
    current = series_in.reshape(series_count * local_length, model_width).astype(jnp.float32)
    gathered_list = []
    stored_list = []
    for layer_index in range(layer_count):
        gathered = (
            lax.all_gather(qkv_weight[layer_index], "fsdp", axis=0, tiled=True),
            lax.all_gather(out_weight[layer_index], "fsdp", axis=0, tiled=True),
            lax.all_gather(up_weight[layer_index], "fsdp", axis=0, tiled=True),
            lax.all_gather(down_weight[layer_index], "fsdp", axis=0, tiled=True),
            lax.all_gather(norm_gains[layer_index], "fsdp", axis=1, tiled=True),
            lax.all_gather(up_bias[layer_index], "fsdp", axis=0, tiled=True),
            lax.all_gather(down_bias[layer_index], "fsdp", axis=0, tiled=True),
            lax.all_gather(query_scale[layer_index], "fsdp", axis=0, tiled=True),
        )
        current, stored = forward_layer(
            current, gathered, allowed, series_count, local_length, total_length
        )
        gathered_list.append(gathered)
        stored_list.append(stored)
    series_out = current.reshape(series_count, local_length, model_width).astype(jnp.bfloat16)
    upstream = cotangent.reshape(series_count * local_length, model_width).astype(jnp.float32)
    owned_list = [None] * layer_count
    for layer_index in reversed(range(layer_count)):
        gathered = (
            lax.all_gather(qkv_weight[layer_index], "fsdp", axis=0, tiled=True),
            lax.all_gather(out_weight[layer_index], "fsdp", axis=0, tiled=True),
            lax.all_gather(up_weight[layer_index], "fsdp", axis=0, tiled=True),
            lax.all_gather(down_weight[layer_index], "fsdp", axis=0, tiled=True),
            lax.all_gather(norm_gains[layer_index], "fsdp", axis=1, tiled=True),
            lax.all_gather(up_bias[layer_index], "fsdp", axis=0, tiled=True),
            lax.all_gather(down_bias[layer_index], "fsdp", axis=0, tiled=True),
            lax.all_gather(query_scale[layer_index], "fsdp", axis=0, tiled=True),
        )
        upstream, layer_grads = backward_layer(
            upstream,
            gathered,
            stored_list[layer_index],
            allowed,
            series_count,
            local_length,
            total_length,
        )
        shares = (
            lax.psum_scatter(
                layer_grads[0].astype(jnp.bfloat16), "fsdp", scatter_dimension=0, tiled=True
            ).astype(jnp.float32),
            lax.psum_scatter(
                layer_grads[1].astype(jnp.bfloat16), "fsdp", scatter_dimension=0, tiled=True
            ).astype(jnp.float32),
            lax.psum_scatter(
                layer_grads[2].astype(jnp.bfloat16), "fsdp", scatter_dimension=0, tiled=True
            ).astype(jnp.float32),
            lax.psum_scatter(
                layer_grads[3].astype(jnp.bfloat16), "fsdp", scatter_dimension=0, tiled=True
            ).astype(jnp.float32),
            lax.psum_scatter(
                layer_grads[4].astype(jnp.bfloat16), "fsdp", scatter_dimension=1, tiled=True
            ).astype(jnp.float32),
            lax.psum_scatter(
                layer_grads[5].astype(jnp.bfloat16), "fsdp", scatter_dimension=0, tiled=True
            ).astype(jnp.float32),
            lax.psum_scatter(
                layer_grads[6].astype(jnp.bfloat16), "fsdp", scatter_dimension=0, tiled=True
            ).astype(jnp.float32),
            lax.psum_scatter(
                layer_grads[7].astype(jnp.bfloat16), "fsdp", scatter_dimension=0, tiled=True
            ).astype(jnp.float32),
        )
        shares = (
            lax.psum(shares[0].astype(jnp.bfloat16), ("replica", "seq")).astype(jnp.float32),
            lax.psum(shares[1].astype(jnp.bfloat16), ("replica", "seq")).astype(jnp.float32),
            lax.psum(shares[2].astype(jnp.bfloat16), ("replica", "seq")).astype(jnp.float32),
            lax.psum(shares[3].astype(jnp.bfloat16), ("replica", "seq")).astype(jnp.float32),
            lax.psum(shares[4].astype(jnp.bfloat16), ("replica", "seq")).astype(jnp.float32),
            lax.psum(shares[5].astype(jnp.bfloat16), ("replica", "seq")).astype(jnp.float32),
            lax.psum(shares[6].astype(jnp.bfloat16), ("replica", "seq")).astype(jnp.float32),
            lax.psum(shares[7].astype(jnp.bfloat16), ("replica", "seq")).astype(jnp.float32),
        )
        owned_list[layer_index] = shares
    stacked = [
        jnp.stack([owned_list[layer_index][member_index] for layer_index in range(layer_count)])
        for member_index in range(8)
    ]
    input_grad = upstream.reshape(series_count, local_length, model_width).astype(jnp.bfloat16)
    return (
        series_out,
        input_grad,
        stacked[0],
        stacked[1],
        stacked[2],
        stacked[3],
        stacked[4],
        stacked[5],
        stacked[6],
        stacked[7],
    )


def solution(mesh):
    return jax.shard_map(
        shards,
        mesh=mesh,
        in_specs=(
            P(("replica", "fsdp"), "seq", None),
            P(("replica", "fsdp"), "seq", None),
            P(None, "fsdp", None),
            P(None, "fsdp", None),
            P(None, "fsdp", None),
            P(None, "fsdp", None),
            P(None, None, "fsdp"),
            P(None, "fsdp"),
            P(None, "fsdp"),
            P(None, "fsdp"),
            P(("replica", "fsdp")),
            P(("replica", "fsdp"), None),
            P(("replica", "fsdp")),
        ),
        out_specs=(
            P(("replica", "fsdp"), "seq", None),
            P(("replica", "fsdp"), "seq", None),
            P(None, "fsdp", None),
            P(None, "fsdp", None),
            P(None, "fsdp", None),
            P(None, "fsdp", None),
            P(None, None, "fsdp"),
            P(None, "fsdp"),
            P(None, "fsdp"),
            P(None, "fsdp"),
        ),
        check_vma=False,
    )
```

profile of v0, /device:TPU:0, one launch (start us, length us, event | category | flops | bytes accessed | tf_op | source)
XLA Modules:
  0.0 1406.5 jit_solution(13420251808383852536)
XLA Ops:
  10.7 17.4 %all-gather = bf16[1,2,1280]{1,0,2:T(2,128)(2,1)S(1)} all-gather(bf16[1,2,160]{1,0,2:T(2,128)(2,1)S(1)} %copy.71), channel_id=2, replica_groups=mesh['replica'=2,'fsdp'=8,'seq'=2] {'fsdp'}, dimensions={2}, use_global_device_ids=true | all-gather | bytes 5760 | tf_op jit(solution)/shard_map/all_gather | solution.py:265
  28.9 20.9 %fusion.139 = (f32[1280]{0:T(1024)S(1)}, f32[1280]{0:T(1024)S(1)}) fusion(bf16[1,2,1280]{1,0,2:T(2,128)(2,1)S(1)} %all-gather), kind=kLoop, calls=%fused_computation.149 | loop fusion | flops 2560 | bytes 15360 | tf_op jit(solution)/shard_map/mul | solution.py:41
  49.9 58.0 %all-gather.31.cloned.1.call-done = bf16[1,1280,3840]{2,1,0:T(8,128)(2,1)} async-done(((bf16[1,160,3840]{2,1,0:T(8,128)(2,1)}), bf16[1,1280,3840]{2,1,0:T(8,128)(2,1)}) %all-gather.31.cloned.1.call-update) | async-done | bytes 9830416 | tf_op jit(solution)/shard_map/all_gather | solution.py:261
  131.1 26.5 %all-reduce.13 = (bf16[80]{0:T(256)(128)(2,1)S(1)}, bf16[1280]{0:T(1024)(128)(2,1)S(1)}, bf16[1280]{0:T(1024)(128)(2,1)S(1)}, bf16[80]{0:T(256)(128)(2,1)S(1)}, bf16[1280]{0:T(1024)(128)(2,1)S(1)}) all-reduce(bf16[80]{0:T(256)(128)(2,1)S(1)} %dynamic-update-slice, ...), channel_id=4, replica_groups=mesh['replica'=2,'fsdp'=8,'seq'=2] {'fsdp'}, use_global_device_ids=true, to_apply=%add | all-reduce | flops 4000 | bytes 16000
  157.8 16.3 %all-gather.8 = bf16[1,2,1280]{1,0,2:T(2,128)(2,1)S(1)} all-gather(bf16[1,2,160]{1,0,2:T(2,128)(2,1)S(1)} %copy.72), channel_id=10, replica_groups=mesh['replica'=2,'fsdp'=8,'seq'=2] {'fsdp'}, dimensions={2}, use_global_device_ids=true | all-gather | bytes 5760 | tf_op jit(solution)/shard_map/all_gather | solution.py:265
  179.8 21.0 %fusion.137 = (f32[1280]{0:T(1024)S(1)}, f32[1280]{0:T(1024)S(1)}) fusion(bf16[1,2,1280]{1,0,2:T(2,128)(2,1)S(1)} %all-gather.8), kind=kLoop, calls=%fused_computation.145 | loop fusion | flops 2560 | bytes 15360 | tf_op jit(solution)/shard_map/mul | solution.py:41
  215.3 15.5 %fusion.120 = bf16[16,80,256]{2,1,0:T(8,128)(2,1)} fusion(bf16[16,80,512]{2,1,0:T(8,128)(2,1)S(1)} %bitcast.276, f32[16,256,512]{2,1,0:T(8,128)S(1)} %get-tuple-element.91, f32[16,256]{1,0:T(8,128)S(1)} %fusion.8, f32[16,256]{1,0:T(8,128)S(1)} %get-tuple-element.90, pred[256,512]{1,0:T(8,128)(4,1)S(1)} %fusion.149), kind=kOutput, calls=%fused_computation.101 | convolution fusion | flops 344260608 | bytes 10518528 | tf_op jit(solution)/shard_map/bhqk,bhek->bheq/dot_general | solution.py:81
  243.2 35.7 %all-gather.37.cloned.1.call-done = bf16[1,1280,1280]{2,1,0:T(8,128)(2,1)} async-done(((bf16[1,160,1280]{2,1,0:T(8,128)(2,1)}), bf16[1,1280,1280]{2,1,0:T(8,128)(2,1)}) %all-gather.37.cloned.1.call-update) | async-done | bytes 3276816 | tf_op jit(solution)/shard_map/all_gather | solution.py:264
  282.9 90.4 %all-gather.39.cloned.1.call-done = bf16[1,1280,3840]{2,1,0:T(8,128)(2,1)} async-done(((bf16[1,160,3840]{2,1,0:T(8,128)(2,1)}), bf16[1,1280,3840]{2,1,0:T(8,128)(2,1)}) %all-gather.39.cloned.1.call-update) | async-done | bytes 9830416 | tf_op jit(solution)/shard_map/all_gather | solution.py:261
  389.5 31.1 %all-gather.29.cloned.1.call-done = bf16[1,2560,512]{1,2,0:T(8,128)(2,1)} async-done(((bf16[1,2560,256]{1,2,0:T(8,128)(2,1)}), bf16[1,2560,512]{1,2,0:T(8,128)(2,1)}) %all-gather.29.cloned.1.call-update) | async-done | bytes 2621456 | tf_op jit(solution)/shard_map/all_gather | solution.py:71
  439.0 22.6 %all-gather.41.cloned.1.call-done = bf16[1,1280,1280]{2,1,0:T(8,128)(2,1)} async-done(((bf16[1,160,1280]{2,1,0:T(8,128)(2,1)}), bf16[1,1280,1280]{2,1,0:T(8,128)(2,1)}) %all-gather.41.cloned.1.call-update) | async-done | bytes 3276816 | tf_op jit(solution)/shard_map/all_gather | solution.py:262
  466.3 35.2 %all-gather.43.cloned.1.call-done = bf16[1,1280,1280]{2,1,0:T(8,128)(2,1)} async-done(((bf16[1,160,1280]{2,1,0:T(8,128)(2,1)}), bf16[1,1280,1280]{2,1,0:T(8,128)(2,1)}) %all-gather.43.cloned.1.call-update) | async-done | bytes 3276816 | tf_op jit(solution)/shard_map/all_gather | solution.py:263
  506.1 35.2 %all-gather.45.cloned.1.call-done = bf16[1,1280,1280]{2,1,0:T(8,128)(2,1)} async-done(((bf16[1,160,1280]{2,1,0:T(8,128)(2,1)}), bf16[1,1280,1280]{2,1,0:T(8,128)(2,1)}) %all-gather.45.cloned.1.call-update) | async-done | bytes 3276816 | tf_op jit(solution)/shard_map/all_gather | solution.py:264
  560.3 7.1 multiply_reduce_fusion.1
  580.0 16.4 %reduce-scatter.21.cloned.1.call-done = f32[1,1280,256]{2,1,0:T(8,128)} async-done(((f32[1,1280,512]{2,1,0:T(8,128)}), f32[1,1280,256]{2,1,0:T(8,128)}) %reduce-scatter.21.cloned.1.call-update) | async-done | bytes 1310736 | tf_op jit(solution)/shard_map/reduce_scatter | solution.py:190
  598.7 37.6 %reduce-scatter.19.cloned.1.call-done = f32[1,1280,256]{2,1,0:T(8,128)} async-done(((f32[1,1280,512]{2,1,0:T(8,128)}), f32[1,1280,256]{2,1,0:T(8,128)}) %reduce-scatter.19.cloned.1.call-update) | async-done | bytes 1310736 | tf_op jit(solution)/shard_map/reduce_scatter | solution.py:184
  637.7 7.2 multiply_reduce_fusion.5
  706.9 8.1 convolution_convert_fusion
  722.4 20.2 %reduce-scatter.23.cloned.1.call-done = f32[1,1280,256]{2,1,0:T(8,128)} async-done(((f32[1,1280,512]{2,1,0:T(8,128)}), f32[1,1280,256]{2,1,0:T(8,128)}) %reduce-scatter.23.cloned.1.call-update) | async-done | bytes 1310736 | tf_op jit(solution)/shard_map/reduce_scatter | solution.py:184
  751.8 7.7 fusion.130
  760.5 25.6 %reduce-scatter.37.cloned.1.call-done = bf16[160,1280]{1,0:T(8,128)(2,1)} async-done(((bf16[1280,1280]{1,0:T(8,128)(2,1)}), bf16[160,1280]{1,0:T(8,128)(2,1)}) %reduce-scatter.37.cloned.1.call-update) | async-done | bytes 409616 | tf_op jit(solution)/shard_map/reduce_scatter | solution.py:305
  786.1 42.4 %reduce-scatter.33.cloned.1.call-done = bf16[160,1280]{1,0:T(8,128)(2,1)} async-done(((bf16[1280,1280]{1,0:T(8,128)(2,1)}), bf16[160,1280]{1,0:T(8,128)(2,1)}) %reduce-scatter.33.cloned.1.call-update) | async-done | bytes 409616 | tf_op jit(solution)/shard_map/reduce_scatter | solution.py:302
  828.6 42.4 %reduce-scatter.41.cloned.1.call-done = bf16[160,1280]{1,0:T(8,128)(2,1)} async-done(((bf16[1280,1280]{1,0:T(8,128)(2,1)}), bf16[160,1280]{1,0:T(8,128)(2,1)}) %reduce-scatter.41.cloned.1.call-update) | async-done | bytes 409616 | tf_op jit(solution)/shard_map/reduce_scatter | solution.py:308
  870.9 42.4 %reduce-scatter.39.cloned.1.call-done = bf16[160,1280]{1,0:T(8,128)(2,1)} async-done(((bf16[1280,1280]{1,0:T(8,128)(2,1)}), bf16[160,1280]{1,0:T(8,128)(2,1)}) %reduce-scatter.39.cloned.1.call-update) | async-done | bytes 409616 | tf_op jit(solution)/shard_map/reduce_scatter | solution.py:308
  913.4 42.5 %reduce-scatter.35.cloned.1.call-done = bf16[160,1280]{1,0:T(8,128)(2,1)} async-done(((bf16[1280,1280]{1,0:T(8,128)(2,1)}), bf16[160,1280]{1,0:T(8,128)(2,1)}) %reduce-scatter.35.cloned.1.call-update) | async-done | bytes 409616 | tf_op jit(solution)/shard_map/reduce_scatter | solution.py:305
  955.9 42.4 %reduce-scatter.31.cloned.1.call-done = bf16[160,1280]{1,0:T(8,128)(2,1)} async-done(((bf16[1280,1280]{1,0:T(8,128)(2,1)}), bf16[160,1280]{1,0:T(8,128)(2,1)}) %reduce-scatter.31.cloned.1.call-update) | async-done | bytes 409616 | tf_op jit(solution)/shard_map/reduce_scatter | solution.py:302
  998.3 104.4 %reduce-scatter.29.cloned.1.call-done = bf16[160,3840]{1,0:T(8,128)(2,1)} async-done(((bf16[1280,3840]{1,0:T(8,128)(2,1)}), bf16[160,3840]{1,0:T(8,128)(2,1)}) %reduce-scatter.29.cloned.1.call-update) | async-done | bytes 1228816 | tf_op jit(solution)/shard_map/reduce_scatter | solution.py:299
  1102.7 104.0 %reduce-scatter.27.cloned.1.call-done = bf16[160,3840]{1,0:T(8,128)(2,1)} async-done(((bf16[1280,3840]{1,0:T(8,128)(2,1)}), bf16[160,3840]{1,0:T(8,128)(2,1)}) %reduce-scatter.27.cloned.1.call-update) | async-done | bytes 1228816 | tf_op jit(solution)/shard_map/reduce_scatter | solution.py:299
  1208.5 26.4 %all-reduce.12 = (bf16[1280]{0:T(1024)(128)(2,1)S(1)}, bf16[1280]{0:T(1024)(128)(2,1)S(1)}, bf16[1280]{0:T(1024)(128)(2,1)S(1)}, bf16[1280]{0:T(1024)(128)(2,1)S...) all-reduce(bf16[1280]{0:T(1024)(128)(2,1)S(1)} %dynamic-update-slic, ...), channel_id=17, replica_groups=mesh['replica'=2,'fsdp'=8,'seq'=2] {'fsdp'}, use_global_device_ids=true, to_apply=%add.5 | all-reduce | flops 6560 | bytes 26240
  1243.3 26.8 %reduce-scatter.43.cloned.1.call-done = bf16[160,2]{1,0:T(8,128)(2,1)} async-done(((bf16[1280,2]{1,0:T(8,128)(2,1)}), bf16[160,2]{1,0:T(8,128)(2,1)}) %reduce-scatter.43.cloned.1.call-update) | async-done | bytes 656
  1270.9 10.0 all-reduce.14
  1283.2 107.7 %all-reduce.18.cloned.1.call-done = (bf16[1,160,3840]{2,1,0:T(8,128)(2,1)}, bf16[1,160,3840]{2,1,0:T(8,128)(2,1)}, bf16[1,160,1280]{2,1,0:T(8,128)(2,1)}, bf16[1...) async-done(((bf16[1,160,3840]{2,1,0:T(8,128)(2,1)}, ...) | async-done | bytes 4915216 | tf_op jit(solution)/shard_map/psum | solution.py:325
  (311 shorter events, 237.3 us)
Async XLA Ops:
  7.2 100.7 %all-gather.31.cloned.1.call-start = ((), (), s32[]{:S(2)}) async-start(), calls=%async_computation.28 | async-start | bytes 11059200 | tf_op jit(solution)/shard_map/all_gather | solution.py:261
  10.5 192.0 %all-gather.27.cloned.1.call-start = ((), (), s32[]{:S(2)}) async-start(), calls=%async_computation.14 | async-start | bytes 3932160 | tf_op jit(solution)/shard_map/all_gather | solution.py:71
  28.9 85.6 %copy-start.41 = (f32[256]{0:T(256)}, f32[256]{0:T(256)S(1)}, u32[]{:S(2)}) copy-start(f32[256]{0:T(256)S(1)} %get-tuple-element.75) | copy-start | bytes 3076
  49.9 64.6 %copy-start.39 = (f32[1280]{0:T(1024)}, f32[1280]{0:T(1024)S(1)}, u32[]{:S(2)}) copy-start(f32[1280]{0:T(1024)S(1)} %get-tuple-element.21) | copy-start | bytes 15364
  117.7 113.2 %all-gather.33.cloned.1.call-start = ((), (), s32[]{:S(2)}) async-start(), calls=%async_computation.29 | async-start | bytes 3686400 | tf_op jit(solution)/shard_map/all_gather | solution.py:262
  119.8 119.4 %all-gather.35.cloned.1.call-start = ((), (), s32[]{:S(2)}) async-start(), calls=%async_computation.30 | async-start | bytes 3686400 | tf_op jit(solution)/shard_map/all_gather | solution.py:263
  120.8 158.1 %all-gather.37.cloned.1.call-start = ((), (), s32[]{:S(2)}) async-start(), calls=%async_computation.31 | async-start | bytes 3686400 | tf_op jit(solution)/shard_map/all_gather | solution.py:264
  122.1 251.2 %all-gather.39.cloned.1.call-start = ((), (), s32[]{:S(2)}) async-start(), calls=%async_computation.32 | async-start | bytes 11059200 | tf_op jit(solution)/shard_map/all_gather | solution.py:261
  122.6 297.9 %all-gather.29.cloned.1.call-start = ((), (), s32[]{:S(2)}) async-start(), calls=%async_computation.15 | async-start | bytes 3932160 | tf_op jit(solution)/shard_map/all_gather | solution.py:71
  157.6 21.8 %copy-start.51 = (bf16[80]{0:T(256)(128)(2,1)}, bf16[80]{0:T(256)(128)(2,1)S(1)}, u32[]{:S(2)}) copy-start(bf16[80]{0:T(256)(128)(2,1)S(1)} %get-tuple-element.33) | copy-start | bytes 484
  157.6 21.8 %copy-start.53 = (bf16[80]{0:T(256)(128)(2,1)}, bf16[80]{0:T(256)(128)(2,1)S(1)}, u32[]{:S(2)}) copy-start(bf16[80]{0:T(256)(128)(2,1)S(1)} %get-tuple-element.36) | copy-start | bytes 484
  282.9 97.0 %copy-start.4 = (f32[256,1280]{1,0:T(8,128)}, f32[256,1280]{1,0:T(8,128)S(1)}, u32[]{:S(2)}) copy-start(f32[256,1280]{1,0:T(8,128)S(1)} %get-tuple-element.95) | copy-start | bytes 3932164
  383.0 78.6 %all-gather.41.cloned.1.call-start = ((), (), s32[]{:S(2)}) async-start(), calls=%async_computation.33 | async-start | bytes 3686400 | tf_op jit(solution)/shard_map/all_gather | solution.py:262
  383.7 117.8 %all-gather.43.cloned.1.call-start = ((), (), s32[]{:S(2)}) async-start(), calls=%async_computation.34 | async-start | bytes 3686400 | tf_op jit(solution)/shard_map/all_gather | solution.py:263
  384.5 156.8 %all-gather.45.cloned.1.call-start = ((), (), s32[]{:S(2)}) async-start(), calls=%async_computation.35 | async-start | bytes 3686400 | tf_op jit(solution)/shard_map/all_gather | solution.py:264
  385.1 211.4 %reduce-scatter.21.cloned.1.call-start = ((), (), s32[]{:S(2)}) async-start(), calls=%async_computation.17 | async-start | bytes 3932160 | tf_op jit(solution)/shard_map/reduce_scatter | solution.py:190
  559.9 76.4 %reduce-scatter.19.cloned.1.call-start = ((), (), s32[]{:S(2)}) async-start(), calls=%async_computation.16 | async-start | bytes 3932160 | tf_op jit(solution)/shard_map/reduce_scatter | solution.py:184
  575.0 145.9 %reduce-scatter.25.cloned.1.call-start = ((), (), s32[]{:S(2)}) async-start(), calls=%async_computation.19 | async-start | bytes 3932160 | tf_op jit(solution)/shard_map/reduce_scatter | solution.py:190
  598.7 39.0 %copy-start.5 = (f32[256,1280]{1,0:T(8,128)S(1)}, f32[256,1280]{1,0:T(8,128)}, u32[]{:S(2)}) copy-start(f32[256,1280]{1,0:T(8,128)} %copy-done.4) | copy-start | bytes 3932164
  665.1 77.5 %reduce-scatter.23.cloned.1.call-start = ((), (), s32[]{:S(2)}) async-start(), calls=%async_computation.18 | async-start | bytes 3932160 | tf_op jit(solution)/shard_map/reduce_scatter | solution.py:184
  679.9 106.2 %reduce-scatter.37.cloned.1.call-start = ((), (), s32[]{:S(2)}) async-start(), calls=%async_computation.25 | async-start | bytes 3686400 | tf_op jit(solution)/shard_map/reduce_scatter | solution.py:305
  684.3 144.3 %reduce-scatter.33.cloned.1.call-start = ((), (), s32[]{:S(2)}) async-start(), calls=%async_computation.23 | async-start | bytes 3686400 | tf_op jit(solution)/shard_map/reduce_scatter | solution.py:302
  688.6 182.4 %reduce-scatter.41.cloned.1.call-start = ((), (), s32[]{:S(2)}) async-start(), calls=%async_computation.27 | async-start | bytes 3686400 | tf_op jit(solution)/shard_map/reduce_scatter | solution.py:308
  693.1 220.2 %reduce-scatter.39.cloned.1.call-start = ((), (), s32[]{:S(2)}) async-start(), calls=%async_computation.26 | async-start | bytes 3686400 | tf_op jit(solution)/shard_map/reduce_scatter | solution.py:308
  698.0 257.9 %reduce-scatter.35.cloned.1.call-start = ((), (), s32[]{:S(2)}) async-start(), calls=%async_computation.24 | async-start | bytes 3686400 | tf_op jit(solution)/shard_map/reduce_scatter | solution.py:305
  702.3 296.0 %reduce-scatter.31.cloned.1.call-start = ((), (), s32[]{:S(2)}) async-start(), calls=%async_computation.22 | async-start | bytes 3686400 | tf_op jit(solution)/shard_map/reduce_scatter | solution.py:302
  706.7 396.0 %reduce-scatter.29.cloned.1.call-start = ((), (), s32[]{:S(2)}) async-start(), calls=%async_computation.21 | async-start | bytes 11059200 | tf_op jit(solution)/shard_map/reduce_scatter | solution.py:299
  715.1 491.7 %reduce-scatter.27.cloned.1.call-start = ((), (), s32[]{:S(2)}) async-start(), calls=%async_computation.20 | async-start | bytes 11059200 | tf_op jit(solution)/shard_map/reduce_scatter | solution.py:299
  750.7 489.2 %reduce-scatter.45.cloned.1.call-start = ((), (), s32[]{:S(2)}) async-start(), calls=%async_computation.37 | async-start | bytes 368640
  751.7 518.3 %reduce-scatter.43.cloned.1.call-start = ((), (), s32[]{:S(2)}) async-start(), calls=%async_computation.36 | async-start | bytes 368640
  760.5 630.4 %all-reduce.18.cloned.1.call-start = ((), (), s32[]{:S(2)}) async-start(), calls=%async_computation.38 | async-start | bytes 9830400 | tf_op jit(solution)/shard_map/psum | solution.py:325
  1206.7 28.6 %copy-start.7 = (f32[256,1280]{1,0:T(8,128)S(1)}, f32[256,1280]{1,0:T(8,128)}, u32[]{:S(2)}) copy-start(f32[256,1280]{1,0:T(8,128)} %get-tuple-element.99) | copy-start | bytes 3932164
  (54 other events, 243.6 us)
Sparse Core Ops, SparseCore 0:
  10.6 97.2 all-gather.30
  117.8 37.5 all-gather.26
  157.6 40.0 all-gather.32
  199.8 39.3 all-gather.34
  240.6 38.2 all-gather.36
  280.4 92.8 all-gather.38
  383.1 37.4 all-gather.28
  422.2 39.3 all-gather.40
  463.3 38.2 all-gather.42
  503.0 38.2 all-gather.44
  560.0 36.4 reduce-scatter.20
  598.6 37.5 reduce-scatter.18
  665.2 37.5 reduce-scatter.24
  704.9 37.5 reduce-scatter.22
  744.7 41.3 reduce-scatter.36
  788.4 40.1 reduce-scatter.32
  830.7 40.1 reduce-scatter.40
  873.2 40.1 reduce-scatter.38
  915.7 40.1 reduce-scatter.34
  958.1 40.1 reduce-scatter.30
  1000.6 102.0 reduce-scatter.28
  1105.1 101.5 reduce-scatter.26
  1209.6 28.8 reduce-scatter.44
  1241.3 28.6 reduce-scatter.42
  1274.5 116.3 all-reduce.17
where the time goes:
time: 1420 us; the launch traced here: 1410 us
  waiting for transfers between devices  971 us (68%)
  matrix products  173 us (12%)
  blocking collectives  96.6 us (7%)
  other arithmetic  82.8 us (6%)
  local copies, waits for them, and re-layouts  59.5 us (4%)
  between operations  21.9 us (2%)
    reduce_scatter x2, waiting for transfers between devices, shards(): lax.psum_scatter(layer_grads[0].astype(jnp.bfloat16), 'fsdp', scatter_dim...  208 us
    all_gather x2, waiting for transfers between devices, shards(): lax.all_gather(qkv_weight[layer_index], 'fsdp', axis=0, tiled=True)  148 us
    psum x1, waiting for transfers between devices, shards(): lax.psum(shares[0].astype(jnp.bfloat16), ('replica', 'seq'))  108 us
    reduce_scatter x2, waiting for transfers between devices, shards(): lax.psum_scatter(layer_grads[1].astype(jnp.bfloat16), 'fsdp', scatter_dim...  84.9 us
    reduce_scatter x2, waiting for transfers between devices, shards(): lax.psum_scatter(layer_grads[3].astype(jnp.bfloat16), 'fsdp', scatter_dim...  84.8 us
    all_gather x2, waiting for transfers between devices, shards(): lax.all_gather(down_weight[layer_index], 'fsdp', axis=0, tiled=True)  70.9 us
    reduce_scatter x2, waiting for transfers between devices, shards(): lax.psum_scatter(layer_grads[2].astype(jnp.bfloat16), 'fsdp', scatter_dim...  68.1 us
    reduce_scatter x2, waiting for transfers between devices, backward_layer(): lax.psum_scatter(key_grad.reshape(series_count, model_width, total_length...  57.8 us
  transfers between devices with their start and end apart: 25, of which 21 were waited for; matrix products, arithmetic and copies ran while one was open for 16% of the time, Pallas kernels for 0%

commit v1 on v0

--- a/solution.py
+++ b/solution.py
@@ -1,8 +1,11 @@
+import functools
 import math
 
 import jax
 import jax.numpy as jnp
 from jax import lax
+from jax.experimental import pallas as pl
+from jax.experimental.pallas import tpu as pltpu
 from jax.sharding import PartitionSpec as P
 
 HEADS = 16
@@ -52,6 +55,1099 @@
     return jax.nn.softplus(query_scale.astype(jnp.float32)) * (SOFT_ONE / math.sqrt(HEAD))
 
 
+MESH = pl.DeviceIdType.MESH
+UNITS = 6
+
+
+class Place:
+    def __init__(self, nz):
+        self.nz = nz
+        self.r = lax.axis_index("replica")
+        f = lax.axis_index("fsdp")
+        self.s = lax.axis_index("seq")
+        self.z = lax.div(f, 2)
+        self.c = lax.rem(f, 2)
+        self.f = f
+
+    def x(self):
+        return (self.r, self.f, 1 - self.s)
+
+    def y(self):
+        return (1 - self.r, self.f, self.s)
+
+    def core(self):
+        return (self.r, self.f + 1 - 2 * self.c, self.s)
+
+    def to(self, d):
+        return (self.r, lax.rem(self.z + d, self.nz) * 2 + self.c, self.s)
+
+    def source(self, d):
+        return lax.rem(self.z - d + self.nz, self.nz)
+
+    def greet(self):
+        barrier = pltpu.get_barrier_semaphore()
+        peers = [self.x(), self.y(), self.core()] + [self.to(d) for d in range(1, self.nz)]
+        for peer in peers:
+            pl.semaphore_signal(barrier, inc=1, device_id=peer, device_id_type=MESH)
+        pl.semaphore_wait(barrier, len(peers))
+
+
+def remote(src, dst, send, recv, device):
+    return pltpu.make_async_remote_copy(
+        src_ref=src, dst_ref=dst, send_sem=send, recv_sem=recv, device_id=device, device_id_type=MESH
+    )
+
+
+class Gather:
+    def __init__(
+        self, nz, layers, qkv_ref, out_ref, up_ref, down_ref, small_ref, full_ref, tiny_ref,
+        mine, local_sem, keep_sem, zs, zr, xs, xr, ys, yr, fxs, fxr, fys, fyr, cs, cr, ts, tr,
+    ):
+        self.__dict__.update(locals())
+        self.at = Place(nz)
+        self.shard, self.width = out_ref.shape[1], out_ref.shape[2]
+        self.half, self.wide = self.shard // 2, self.width // 2
+        self.units = layers * UNITS
+        self.hops = nz - 1
+        self.iterations = self.units + self.hops + 2
+
+    def source(self, way, k):
+        return self.at.z - way * k
+
+    def comes(self, way, k):
+        z = self.at.z
+        return z >= k if way > 0 else z + k < self.nz
+
+    def goes(self, way):
+        z = self.at.z
+        return z + 1 < self.nz if way > 0 else z >= 1
+
+    def next(self, way):
+        at = self.at
+        return (at.r, 2 * (at.z + way) + at.c, at.s)
+
+    def slot(self, way, k):
+        return 2 * (k - 1) + (0 if way > 0 else 1)
+
+    def block(self, u, z, c, r, s):
+        row = pl.multiple_of((2 * z + c) * self.shard + r * self.half, 8)
+        col = pl.multiple_of(s * self.wide, 128)
+        return self.full_ref.at[u, pl.ds(row, self.half), pl.ds(col, self.wide)]
+
+    def quarter(self, u, z, c, r, s, part):
+        step = self.half // 2
+        row = pl.multiple_of((2 * z + c) * self.shard + r * self.half + part * step, 8)
+        col = pl.multiple_of(s * self.wide, 128)
+        return self.full_ref.at[u, pl.ds(row, step), pl.ds(col, self.wide)]
+
+    def own(self, u, c):
+        row = pl.multiple_of((2 * self.at.z + c) * self.shard, 8)
+        return self.full_ref.at[u, pl.ds(row, self.shard), :]
+
+    def local(self, layer, k):
+        if k < 3:
+            piece = self.qkv_ref.at[layer, :, pl.ds(k * self.width, self.width)]
+        else:
+            piece = (self.out_ref, self.up_ref, self.down_ref)[k - 3].at[layer]
+        u = layer * UNITS + k
+        return pltpu.make_async_copy(piece, self.mine.at[u], self.local_sem.at[u])
+
+    def keep(self, u):
+        return pltpu.make_async_copy(self.mine.at[u], self.own(u, self.at.c), self.keep_sem.at[u])
+
+    def z_copy(self, u, way, k):
+        at, n = self.at, self.slot(way, k)
+        piece = self.block(u, self.source(way, k - 1), at.c, at.r, at.s)
+        held = piece
+        if k == 1:
+            row = pl.multiple_of(at.r * self.half, 16)
+            held = self.mine.at[u, pl.ds(row, self.half), pl.ds(pl.multiple_of(at.s * self.wide, 128), self.wide)]
+        return remote(held, piece, self.zs.at[u, n], self.zr.at[u, n], self.next(way))
+
+    def z_came(self, u, way, k):
+        at, n = self.at, self.slot(way, k)
+        piece = self.block(u, self.source(way, k), at.c, at.r, at.s)
+        return remote(piece, piece, self.zs.at[u, n], self.zr.at[u, n], self.next(way))
+
+    def x_copy(self, u, way, k):
+        at, n = self.at, self.slot(way, k)
+        piece = self.block(u, self.source(way, k), at.c, at.r, at.s)
+        return remote(piece, piece, self.xs.at[u, n], self.xr.at[u, n], at.x())
+
+    def y_copy(self, u, way, k):
+        at, n = self.at, self.slot(way, k)
+        piece = self.block(u, self.source(way, k), at.c, at.r, at.s)
+        return remote(piece, piece, self.ys.at[u, n], self.yr.at[u, n], at.y())
+
+    def fx_copy(self, u, way, k):
+        at, n = self.at, self.slot(way, k)
+        piece = self.quarter(u, self.source(way, k), at.c, 1 - at.r, at.s, 1)
+        return remote(piece, piece, self.fxs.at[u, n], self.fxr.at[u, n], at.x())
+
+    def fy_copy(self, u, way, k):
+        at, n = self.at, self.slot(way, k)
+        piece = self.quarter(u, self.source(way, k), at.c, at.r, 1 - at.s, 0)
+        return remote(piece, piece, self.fys.at[u, n], self.fyr.at[u, n], at.y())
+
+    def core_own(self, u):
+        own, n = self.own(u, self.at.c), 8 * self.hops
+        return remote(self.mine.at[u], own, self.cs.at[u, n], self.cr.at[u, n], self.at.core())
+
+    def core_copy(self, u, way, k, which):
+        at = self.at
+        r = at.r if which in (0, 1) else 1 - at.r
+        s = at.s if which in (0, 2) else 1 - at.s
+        piece = self.block(u, self.source(way, k), at.c, r, s)
+        n = 4 * self.slot(way, k) + which
+        return remote(piece, piece, self.cs.at[u, n], self.cr.at[u, n], at.core())
+
+    def tiny(self, d):
+        piece = self.tiny_ref.at[self.at.f]
+        return remote(piece, piece, self.ts.at[d - 1], self.tr.at[d - 1], self.at.to(d))
+
+    def tiny_core(self, d):
+        piece, n = self.tiny_ref.at[2 * self.at.source(d) + self.at.c], self.nz - 1 + d
+        return remote(piece, piece, self.ts.at[n], self.tr.at[n], self.at.core())
+
+    def begin(self):
+        self.tiny_ref[self.at.f] = self.small_ref[...]
+        for layer in range(self.layers):
+            for k in range(UNITS):
+                self.local(layer, k).start()
+        self.at.greet()
+        for d in range(1, self.nz):
+            self.tiny(d).start()
+        self.tiny_core(0).start()
+
+    def tiny_pass(self):
+        for d in range(1, self.nz):
+            self.tiny(d).wait_recv()
+            self.tiny_core(d).start()
+
+    def tiny_ready(self):
+        for d in range(self.nz):
+            self.tiny_core(d).wait_recv()
+
+    def tiny_done(self):
+        for d in range(1, self.nz):
+            self.tiny(d).wait_send()
+        for d in range(self.nz):
+            self.tiny_core(d).wait_send()
+
+    def when(self, cond, work):
+        pl.when(cond)(work)
+
+    def first(self, u):
+        pltpu.make_async_copy(self.out_ref.at[0], self.mine.at[u], self.local_sem.at[u]).wait()
+        self.keep(u).start()
+        for way in (1, -1):
+            self.when(self.goes(way), lambda way=way: self.z_copy(u, way, 1).start())
+        self.core_own(u).start()
+
+    def hop(self, u, k):
+        for way in (1, -1):
+            def work(way=way):
+                self.z_came(u, way, k).wait_recv()
+                if k < self.hops:
+                    self.when(self.goes(way), lambda: self.z_copy(u, way, k + 1).start())
+                self.x_copy(u, way, k).start()
+                self.y_copy(u, way, k).start()
+                self.core_copy(u, way, k, 0).start()
+            self.when(self.comes(way, k), work)
+
+    def forward(self, u, k):
+        for way in (1, -1):
+            def work(way=way):
+                self.x_copy(u, way, k).wait_recv()
+                self.fy_copy(u, way, k).start()
+                self.core_copy(u, way, k, 1).start()
+                self.y_copy(u, way, k).wait_recv()
+                self.fx_copy(u, way, k).start()
+                self.core_copy(u, way, k, 2).start()
+            self.when(self.comes(way, k), work)
+
+    def diagonal(self, u, k):
+        for way in (1, -1):
+            def work(way=way):
+                self.fx_copy(u, way, k).wait_recv()
+                self.fy_copy(u, way, k).wait_recv()
+                self.core_copy(u, way, k, 3).start()
+            self.when(self.comes(way, k), work)
+
+    def step(self, i):
+        def stage(lag, work):
+            u = i - lag
+            self.when((u >= 0) & (u < self.units), lambda: work(u))
+
+        stage(0, self.first)
+        for k in range(1, self.hops + 1):
+            stage(k, lambda u, k=k: self.hop(u, k))
+        for k in range(1, self.hops + 1):
+            stage(k + 1, lambda u, k=k: self.forward(u, k))
+        for k in range(1, self.hops + 1):
+            stage(k + 2, lambda u, k=k: self.diagonal(u, k))
+
+    def ready(self, u):
+        self.keep(u).wait()
+        self.core_own(u).wait_recv()
+        for k in range(1, self.hops + 1):
+            for way in (1, -1):
+                def work(way=way, k=k):
+                    for which in range(4):
+                        self.core_copy(u, way, k, which).wait_recv()
+                self.when(self.comes(way, k), work)
+
+    def drain(self, u):
+        self.core_own(u).wait_send()
+        for k in range(1, self.hops + 1):
+            for way in (1, -1):
+                def sent(way=way, k=k):
+                    self.z_copy(u, way, k).wait_send()
+                came = self.goes(way)
+                if k > 1:
+                    came = came & self.comes(way, k - 1)
+                self.when(came, sent)
+
+                def work(way=way, k=k):
+                    for copy in (self.x_copy, self.y_copy, self.fx_copy, self.fy_copy):
+                        copy(u, way, k).wait_send()
+                    for which in range(4):
+                        self.core_copy(u, way, k, which).wait_send()
+                self.when(self.comes(way, k), work)
+
+    def finish(self):
+        @pl.loop(0, self.units)
+        def _(u):
+            self.drain(u)
+
+        self.tiny_done()
+
+
+def gather_scratch(nz, layers, shard, width):
+    units, n = layers * UNITS, 2 * (nz - 1)
+    dma = pltpu.SemaphoreType.DMA
+    return (
+        [pltpu.VMEM((units, shard, width), jnp.bfloat16), dma((units,)), dma((units,))]
+        + [dma((units, n))] * 10
+        + [dma((units, 1 + 4 * n))] * 2
+        + [dma((2 * nz,))] * 2
+    )
+
+
+def dot_nn(a, b):
+    return jnp.dot(a, b, preferred_element_type=jnp.float32)
+
+
+def dot_nt(a, b):
+    return lax.dot_general(a, b, (((1,), (1,)), ((), ())), preferred_element_type=jnp.float32)
+
+
+def dot_tn(a, b):
+    return lax.dot_general(a, b, (((0,), (0,)), ((), ())), preferred_element_type=jnp.float32)
+
+
+ROWS = 128
+
+
+def each_tile(count, body):
+    @pl.loop(0, count // ROWS)
+    def _(i):
+        body(pl.ds(pl.multiple_of(i * ROWS, ROWS), ROWS))
+
+
+def head_rows(h):
+    return pl.ds(pl.multiple_of(h * HEAD, 16), HEAD)
+
+
+def row_norm(values, gain):
+    inverse = lax.rsqrt(jnp.mean(values * values, axis=-1, keepdims=True) + EPSILON)
+    return (values * inverse * gain).astype(jnp.bfloat16)
+
+
+def expand_small(tiny_ref, vec_ref, layers, shard, part):
+    width = vec_ref.shape[1]
+    count = tiny_ref.shape[0]
+    rows, lanes = tiny_ref.shape[1:]
+    line = lax.broadcasted_iota(jnp.int32, (lanes, width), 0)
+    column = lax.broadcasted_iota(jnp.int32, (lanes, width), 1)
+    inner = lax.rem(column, HEAD)
+
+    def place(f, sums):
+        plain, scale = sums
+        piece = tiny_ref[f]
+        hot = jnp.where((column - f * shard == line) & (line < shard), 1.0, 0.0).astype(jnp.bfloat16)
+        spread = jnp.where((inner - f * part == line) & (line < part), 1.0, 0.0).astype(jnp.bfloat16)
+        return plain + dot_nn(piece, hot), scale + dot_nn(piece, spread)
+
+    zero = jnp.zeros((rows, width), jnp.float32)
+    plain, scale = lax.fori_loop(0, count, place, (zero, zero))
+    soft = jnp.maximum(scale, 0.0) + jnp.log(1.0 + jnp.exp(-jnp.abs(scale)))
+    row = lax.broadcasted_iota(jnp.int32, (rows, width), 0)
+    vec_ref[...] = jnp.where(row < 4 * layers, plain, soft * (SOFT_ONE / math.sqrt(HEAD)))
+
+
+def attend(heads, q_ref, k_ref, v_ref, bias_ref, out_ref, lse_ref):
+    queries = q_ref.shape[1]
+
+    @pl.loop(*heads)
+    def _(h):
+        rows = head_rows(h)
+        scores = dot_tn(k_ref[rows, :], q_ref[rows, :]) + bias_ref[:, :queries]
+        top = jnp.max(scores, axis=0, keepdims=True)
+        grown = jnp.exp(scores - top)
+        total = jnp.sum(grown, axis=0, keepdims=True)
+        out = dot_nn(v_ref[rows, :], grown.astype(jnp.bfloat16)) * (1.0 / total)
+        out_ref[rows, :] = out.astype(jnp.bfloat16)
+        lse_ref[h] = top + jnp.log(total)
+
+
+def forward_kernel(nz, layers, part, *refs):
+    series_ref, qkv_ref, out_ref, up_ref, down_ref, small_ref, bias_ref = refs[:7]
+    full_ref, vec_out, series_out = refs[7:10]
+    per = 11
+    saved = [refs[10 + per * l : 10 + per * (l + 1)] for l in range(layers)]
+    refs = refs[10 + per * layers :]
+    names = ("current", "normed_t", "q", "k", "v", "lse", "att", "after", "mixed", "pre", "hidden")
+    held = [dict(zip(names, refs[per * l : per * (l + 1)])) for l in range(layers)]
+    refs = refs[per * layers :]
+    normed, weight, vec, last, tiny_ref, swap_sem, load_sem, save_sem = refs[:8]
+    gather = Gather(
+        nz, layers, qkv_ref, out_ref, up_ref, down_ref, small_ref, full_ref, tiny_ref, *refs[8:]
+    )
+    at = gather.at
+    length = series_ref.shape[0]
+    total = held[0]["normed_t"].shape[1]
+    other = total - length
+
+    own_copy = pltpu.make_async_copy(series_ref, held[0]["current"].at[pl.ds(0, length)], swap_sem.at[0])
+    swap_copy = remote(
+        series_ref, held[0]["current"].at[pl.ds(length, other)], swap_sem.at[1], swap_sem.at[2], at.x()
+    )
+
+    def save(l, n):
+        return pltpu.make_async_copy(held[l][names[n]], saved[l][n], save_sem.at[l, n])
+
+    def fetch(u):
+        gather.ready(u)
+        copy = pltpu.make_async_copy(full_ref.at[u], weight, load_sem.at[0])
+        copy.start()
+        copy.wait()
+
+    def vector(n):
+        return vec[n : n + 1, :]
+
+    def normalize(l):
+        b = held[l]
+        gain = vector(2 * l)
+
+        def body(r):
+            values = row_norm(b["current"][r, :].astype(jnp.float32), gain)
+            normed[r, :] = values
+            b["normed_t"][:, r] = values.T
+        each_tile(total, body)
+        save(l, 1).start()
+
+    def project(l, n):
+        b = held[l]
+        target = b[("q", "k", "v")[n]]
+        fetch(l * UNITS + n)
+
+        def body(r):
+            values = dot_nn(normed[r, :], weight[...])
+            if n == 0:
+                values = values * vector(4 * layers + l)
+            target[:, r] = values.astype(jnp.bfloat16).T
+        each_tile(target.shape[1], body)
+        save(l, 2 + n).start()
+
+    def attention(l, first):
+        b = held[l]
+        heads = (0, HEADS // 2) if first else (HEADS // 2, HEADS)
+        attend(heads, b["q"], b["k"], b["v"], bias_ref, b["att"], b["lse"])
+        if not first:
+            save(l, 5).start()
+            save(l, 6).start()
+
+    def output(l):
+        b = held[l]
+        fetch(l * UNITS + 3)
+        gain = vector(2 * l + 1)
+
+        def body(r):
+            after = b["current"][r, :].astype(jnp.float32) + dot_tn(b["att"][:, r], weight[...])
+            b["after"][r, :] = after
+            b["mixed"][r, :] = row_norm(after, gain)
+        each_tile(b["after"].shape[0], body)
+        save(l, 7).start()
+        save(l, 8).start()
+
+    def expand(l):
+        b = held[l]
+        fetch(l * UNITS + 4)
+        bias = vector(2 * layers + l)
+
+        def body(r):
+            pre = dot_nn(b["mixed"][r, :], weight[...]) + bias
+            b["pre"][r, :] = pre
+            b["hidden"][r, :] = (pre * (1.0 / (1.0 + jnp.exp(-pre)))).astype(jnp.bfloat16)
+        each_tile(b["pre"].shape[0], body)
+        save(l, 9).start()
+        save(l, 10).start()
+
+    def contract(l):
+        b = held[l]
+        fetch(l * UNITS + 5)
+        bias = vector(3 * layers + l)
+
+        def body(r):
+            values = b["after"][r, :] + (dot_nn(b["hidden"][r, :], weight[...]) + bias)
+            if l + 1 < layers:
+                held[l + 1]["current"][r, :] = values
+            else:
+                last[r, :] = values.astype(jnp.bfloat16)
+        each_tile(b["after"].shape[0], body)
+        if l + 1 < layers:
+            save(l + 1, 0).start()
+            normalize(l + 1)
+        else:
+            pltpu.make_async_copy(last, series_out, swap_sem.at[3]).start()
+
+    tasks = {}
+
+    def add(i, work):
+        tasks.setdefault(i, []).append(work)
+
+    lag = gather.hops + 2
+
+    def early():
+        gather.tiny_pass()
+        gather.tiny_ready()
+        expand_small(tiny_ref, vec, layers, gather.shard, part)
+        pltpu.make_async_copy(vec, vec_out, swap_sem.at[4]).start()
+
+    def begin():
+        own_copy.wait()
+        swap_copy.wait_recv()
+        save(0, 0).start()
+        normalize(0)
+
+    add(1, early)
+    add(2, begin)
+    for l in range(layers):
+        base = l * UNITS + lag
+        for n in range(3):
+            add(base + n, lambda l=l, n=n: project(l, n))
+        add(base + 2, lambda l=l: attention(l, True))
+        add(base + 3, lambda l=l: attention(l, False))
+        add(base + 3, lambda l=l: output(l))
+        add(base + 4, lambda l=l: expand(l))
+        add(base + 5, lambda l=l: contract(l))
+
+    own_copy.start()
+    gather.begin()
+    swap_copy.start()
+
+    @pl.loop(0, gather.iterations)
+    def _(i):
+        gather.step(i)
+        for when, work in sorted(tasks.items()):
+            @pl.when(i == when)
+            def _(work=work):
+                for one in work:
+                    one()
+
+    swap_copy.wait_send()
+    pltpu.make_async_copy(last, series_out, swap_sem.at[3]).wait()
+    pltpu.make_async_copy(vec, vec_out, swap_sem.at[4]).wait()
+    for l in range(layers):
+        for n in range(per):
+            save(l, n).wait()
+    gather.finish()
+
+
+def saved_shapes(layers, length, total, width):
+    low, wide = jnp.bfloat16, jnp.float32
+    shapes = []
+    for l in range(layers):
+        count = length if l == layers - 1 else total
+        kind = low if l == 0 else wide
+        shapes.append(
+            [
+                ((total, width), kind),
+                ((width, total), low),
+                ((width, count), low),
+                ((width, total), low),
+                ((width, total), low),
+                ((HEADS, 1, count), wide),
+                ((width, count), low),
+                ((count, width), wide),
+                ((count, width), low),
+                ((count, width), wide),
+                ((count, width), low),
+            ]
+        )
+    return shapes
+
+
+def forward_pass(nz, series, qkv_weight, out_weight, up_weight, down_weight, small, bias, part):
+    layers, shard, width = out_weight.shape
+    length, total = series.shape[0], bias.shape[0]
+    units = layers * UNITS
+    low, wide = jnp.bfloat16, jnp.float32
+    shapes = [one for group in saved_shapes(layers, length, total, width) for one in group]
+    dma = pltpu.SemaphoreType.DMA
+    anywhere = pl.BlockSpec(memory_space=pl.ANY)
+    inside = pl.BlockSpec(memory_space=pltpu.VMEM)
+    count = 2 * nz
+    results = pl.pallas_call(
+        functools.partial(forward_kernel, nz, layers, part),
+        out_shape=(
+            jax.ShapeDtypeStruct((units, count * shard, width), low),
+            jax.ShapeDtypeStruct((small.shape[0], width), wide),
+            jax.ShapeDtypeStruct((length, width), low),
+        )
+        + tuple(jax.ShapeDtypeStruct(*one) for one in shapes),
+        in_specs=[anywhere] * 5 + [inside] * 2,
+        out_specs=(anywhere,) * (3 + len(shapes)),
+        scratch_shapes=[pltpu.VMEM(*one) for one in shapes]
+        + [
+            pltpu.VMEM((total, width), low),
+            pltpu.VMEM((width, width), low),
+            pltpu.VMEM((small.shape[0], width), wide),
+            pltpu.VMEM((length, width), low),
+            pltpu.VMEM((count,) + small.shape, low),
+            dma((5,)),
+            dma((1,)),
+            dma((layers, 11)),
+        ]
+        + gather_scratch(nz, layers, shard, width),
+        compiler_params=pltpu.CompilerParams(
+            collective_id=1, has_side_effects=True, vmem_limit_bytes=60 << 20
+        ),
+    )(series, qkv_weight, out_weight, up_weight, down_weight, small, bias)
+    full, vec, out = results[:3]
+    saved = [results[3 + 11 * l : 14 + 11 * l] for l in range(layers)]
+    return full, vec, out, saved
+
+
+def pair_bias(pad_length, span_starts, span_count, length):
+    s = lax.axis_index("seq")
+    place = jnp.arange(length, dtype=jnp.int32)
+    position = jnp.concatenate([s * length + place, (1 - s) * length + place])
+    key, query = position[:, None], position[None, :]
+    seen = key <= query
+    for slot in range(span_starts.shape[1]):
+        start = span_starts[0, slot]
+        inside = (position >= start) & (position < start + SPAN) & (slot < span_count[0])
+        seen = seen | inside[:, None] & inside[None, :]
+    allowed = (seen & (key >= pad_length[0])) | (key == query)
+    return jnp.where(allowed, 0.0, NEG_FILL).astype(jnp.float32)
+
+
+class Reduce:
+    def __init__(
+        self, nz, units, full_ref, tiny, tiny_out, grads, held, bx, by, dx, dy, cz, total, tiny_in,
+        as_, ar, bs, br, ds_, dr, zs, zr, ls, ps, pr, ts, tr, free,
+    ):
+        self.__dict__.update(locals())
+        self.at = Place(nz)
+        self.slots, _, self.shard, self.width = held.shape
+        self.half, self.wide, self.low = self.shard // 2, self.width // 2, nz // 2
+        self.steps = range(1, nz)
+        self.iterations = units + 6
+
+    def rows(self, r):
+        return pl.ds(pl.multiple_of(r * self.half, 16), self.half)
+
+    def cols(self, s):
+        return pl.ds(pl.multiple_of(s * self.wide, 128), self.wide)
+
+    def slot(self, u):
+        return lax.rem(u, self.slots)
+
+    def a_copy(self, u):
+        return remote(
+            self.grads.at[:, 1 - self.at.c], self.held.at[self.slot(u)], self.as_.at[u], self.ar.at[u], self.at.core()
+        )
+
+    def bx_copy(self, u):
+        piece = self.held.at[self.slot(u), pl.ds(0, self.low), :, self.cols(1 - self.at.s)]
+        return remote(piece, self.bx.at[u], self.bs.at[u, 0], self.br.at[u, 0], self.at.x())
+
+    def by_copy(self, u):
+        piece = self.held.at[self.slot(u), pl.ds(self.low, self.low), self.rows(1 - self.at.r), :]
+        return remote(piece, self.by.at[u], self.bs.at[u, 1], self.br.at[u, 1], self.at.y())
+
+    def dy_copy(self, u):
+        piece = self.held.at[self.slot(u), pl.ds(0, self.low), self.rows(1 - self.at.r), self.cols(self.at.s)]
+        return remote(piece, self.dy.at[u], self.ds_.at[u, 0], self.dr.at[u, 0], self.at.y())
+
+    def dx_copy(self, u):
+        piece = self.held.at[self.slot(u), pl.ds(self.low, self.low), self.rows(self.at.r), self.cols(1 - self.at.s)]
+        return remote(piece, self.dx.at[u], self.ds_.at[u, 1], self.dr.at[u, 1], self.at.x())
+
+    def z_copy(self, u, d):
+        at = self.at
+        target = lax.rem(at.z + d, self.nz)
+        piece = self.held.at[self.slot(u), target, self.rows(at.r), self.cols(at.s)]
+        return remote(piece, self.cz.at[u, d - 1], self.zs.at[u, d - 1], self.zr.at[u, d - 1], at.to(d))
+
+    def final(self, u, r, s):
+        return self.full_ref.at[u, self.rows(r), self.cols(s)]
+
+    def part(self, u, r, s, p):
+        step = self.half // 2
+        return self.full_ref.at[u, pl.ds(pl.multiple_of(r * self.half + p * step, 8), step), self.cols(s)]
+
+    def put_copy(self, u):
+        return pltpu.make_async_copy(self.total.at[u], self.final(u, self.at.r, self.at.s), self.ls.at[u])
+
+    def px_copy(self, u):
+        spot = self.final(u, self.at.r, self.at.s)
+        return remote(self.total.at[u], spot, self.ps.at[u, 0], self.pr.at[u, 0], self.at.x())
+
+    def py_copy(self, u):
+        spot = self.final(u, self.at.r, self.at.s)
+        return remote(self.total.at[u], spot, self.ps.at[u, 1], self.pr.at[u, 1], self.at.y())
+
+    def gx_copy(self, u):
+        piece = self.part(u, 1 - self.at.r, self.at.s, 1)
+        return remote(piece, piece, self.ps.at[u, 2], self.pr.at[u, 2], self.at.x())
+
+    def gy_copy(self, u):
+        piece = self.part(u, self.at.r, 1 - self.at.s, 0)
+        return remote(piece, piece, self.ps.at[u, 3], self.pr.at[u, 3], self.at.y())
+
+    def plus(self, *values):
+        return sum(v.astype(jnp.float32) for v in values).astype(jnp.bfloat16)
+
+    def each(self, count, body):
+        @pl.loop(0, count // 16)
+        def _(i):
+            body(i * 16)
+
+    def line(self, row):
+        return pl.ds(pl.multiple_of(row, 16), 16)
+
+    def a_start(self, u):
+        @pl.when(u >= self.slots)
+        def _():
+            pl.semaphore_wait(self.free, 1)
+        self.a_copy(u).start()
+
+    def a_stage(self, u):
+        held, slot, c = self.held, self.slot(u), self.at.c
+        self.a_copy(u).wait_recv()
+        for z in range(self.nz):
+            def add(row, z=z):
+                row = self.line(row)
+                held[slot, z, row, :] = self.plus(held[slot, z, row, :], self.grads[z, c, row, :])
+            self.each(self.shard, add)
+            if z == self.low - 1:
+                self.bx_copy(u).start()
+        self.by_copy(u).start()
+        self.a_copy(u).wait_send()
+
+    def b_stage(self, u):
+        held, slot, at = self.held, self.slot(u), self.at
+        self.bx_copy(u).wait_recv()
+        self.bx_copy(u).wait_send()
+        for z in range(self.low):
+            def add(row, z=z):
+                row, mine = self.line(row), self.cols(at.s)
+                held[slot, z, row, mine] = self.plus(held[slot, z, row, mine], self.bx[u, z, row, :])
+            self.each(self.shard, add)
+        self.dy_copy(u).start()
+        self.by_copy(u).wait_recv()
+        self.by_copy(u).wait_send()
+        for z in range(self.low):
+            def add(row, z=z):
+                spot, row = self.line(row), self.line(at.r * self.half + row)
+                z2 = self.low + z
+                held[slot, z2, row, :] = self.plus(held[slot, z2, row, :], self.by[u, z, spot, :])
+            self.each(self.half, add)
+        self.dx_copy(u).start()
+
+    def d_stage(self, u):
+        held, slot, at = self.held, self.slot(u), self.at
+        for copy in (self.dy_copy(u), self.dx_copy(u)):
+            copy.wait_recv()
+            copy.wait_send()
+        for z in range(self.nz):
+            came = self.dy if z < self.low else self.dx
+
+            def add(row, z=z, came=came):
+                spot, row = self.line(row), self.line(at.r * self.half + row)
+                mine = self.cols(at.s)
+                held[slot, z, row, mine] = self.plus(held[slot, z, row, mine], came[u, z % self.low, spot, :])
+            self.each(self.half, add)
+        for d in self.steps:
+            self.z_copy(u, d).start()
+
+    def z_stage(self, u):
+        slot, at = self.slot(u), self.at
+        for d in self.steps:
+            self.z_copy(u, d).wait_recv()
+            self.z_copy(u, d).wait_send()
+
+        def add(row):
+            spot, row = self.line(row), self.line(at.r * self.half + row)
+            came = [self.cz[u, d - 1, spot, :] for d in self.steps]
+            self.total[u, spot, :] = self.plus(self.held[slot, at.z, row, self.cols(at.s)], *came)
+        self.each(self.half, add)
+
+        @pl.when(u + self.slots < self.units)
+        def _():
+            pl.semaphore_signal(self.free, inc=1, device_id=at.core(), device_id_type=MESH)
+        self.put_copy(u).start()
+        self.px_copy(u).start()
+        self.py_copy(u).start()
+
+    def forward(self, u):
+        self.px_copy(u).wait_recv()
+        self.gy_copy(u).start()
+        self.py_copy(u).wait_recv()
+        self.gx_copy(u).start()
+
+    def close(self, u):
+        self.put_copy(u).wait()
+        self.px_copy(u).wait_send()
+        self.py_copy(u).wait_send()
+        self.gx_copy(u).wait()
+        self.gy_copy(u).wait()
+
+    def step(self, i):
+        def stage(lag, work):
+            u = i - lag
+            pl.when((u >= 0) & (u < self.units))(lambda: work(u))
+
+        stage(0, self.a_start)
+        stage(2, self.d_stage)
+        stage(3, self.z_stage)
+        stage(4, self.forward)
+        stage(0, self.a_stage)
+        stage(1, self.b_stage)
+        stage(5, self.close)
+
+    def tiny_copy(self, n, peer):
+        return remote(self.tiny, self.tiny_in.at[n], self.ts.at[n], self.tr.at[n], peer)
+
+    def tiny_z(self, d):
+        return remote(self.tiny, self.tiny_in.at[2 + d], self.ts.at[2 + d], self.tr.at[2 + d], self.at.to(d))
+
+    def tiny_step(self, n):
+        peers = (self.at.core(), self.at.x(), self.at.y())
+        if 0 < n <= 3:
+            copy = self.tiny_copy(n - 1, peers[n - 1])
+            copy.wait()
+            self.tiny[...] = self.tiny[...] + self.tiny_in[n - 1]
+        if n < 3:
+            self.tiny_copy(n, peers[n]).start()
+        if n == 3:
+            for d in self.steps:
+                self.tiny_z(d).start()
+        if n == 4:
+            for d in self.steps:
+                self.tiny_z(d).wait()
+            self.tiny_out[...] = self.tiny[...] + sum(self.tiny_in[2 + d] for d in self.steps)
+
+
+def backward_kernel(nz, layers, length, total, *refs):
+    cot_ref, full_ref, vec, bias_ref = refs[:4]
+    per = 11
+    saved = [refs[4 + per * l : 4 + per * (l + 1)] for l in range(layers)]
+    refs = refs[4 + per * layers :]
+    share_ref, tiny_out, input_ref = refs[:3]
+    (
+        up, wide_a, wide_b, hidden, mixed, pre_low, low, q, k, v, att, do, lse, weight, came, sent,
+        load_sem, weight_sem, x_sem, tiny, grads,
+    ) = refs[3:24]
+    units = layers * UNITS
+    reduce = Reduce(nz, units, share_ref, tiny, tiny_out, grads, *refs[24:])
+    at = reduce.at
+    width = up.shape[1]
+    wide, half_z = width // 2, nz // 2
+    shard = reduce.shard
+    names = ("current", "normed_t", "q", "k", "v", "lse", "att", "after", "mixed", "pre", "hidden")
+    homes = dict(
+        normed_t=att, q=q, k=k, v=v, lse=lse, att=att, after=wide_b, mixed=mixed, pre=wide_a, hidden=hidden
+    )
+
+    def load(l, name):
+        n = names.index(name)
+        source = saved[l][n]
+        home = homes.get(name, hidden if source.dtype == jnp.bfloat16 else wide_b)
+        if home.shape != source.shape:
+            if len(source.shape) == 3:
+                home = home.at[:, :, pl.ds(0, source.shape[2])]
+            elif source.shape[0] != home.shape[0]:
+                home = home.at[pl.ds(0, source.shape[0]), :]
+            else:
+                home = home.at[:, pl.ds(0, source.shape[1])]
+        return pltpu.make_async_copy(source, home, load_sem.at[l, n])
+
+    def fetch(u):
+        return pltpu.make_async_copy(full_ref.at[u], weight, weight_sem.at[0])
+
+    def fill(product):
+        @pl.loop(0, 2)
+        def _(i):
+            @pl.loop(0, 2)
+            def _(j):
+                r = pl.ds(pl.multiple_of(i * wide, 128), wide)
+                c = pl.ds(pl.multiple_of(j * wide, 128), wide)
+                value = product(r, c).astype(jnp.bfloat16).reshape(half_z, 2, shard, wide)
+                grads[pl.ds(i * half_z, half_z), :, :, c] = value
+
+    def vector(n):
+        return vec[n : n + 1, :]
+
+    def gather_row(n, values):
+        tiny[n : n + 1, :] = tiny[n : n + 1, :] + jnp.sum(values, axis=0, keepdims=True)
+
+    def norm_tile(values, gain, w, n):
+        inverse = lax.rsqrt(jnp.mean(values * values, axis=-1, keepdims=True) + EPSILON)
+        scaled = w * gain
+        inner = jnp.mean(values * scaled, axis=-1, keepdims=True)
+        gather_row(n, w * values * inverse)
+        return inverse * scaled - values * (inverse * inverse * inverse) * inner
+
+    def count(l):
+        return length if l == layers - 1 else total
+
+    def next_load(l, *which):
+        if l > 0:
+            for name in which:
+                load(l - 1, name).start()
+
+    def down(l):
+        m = count(l)
+        load(l, "hidden").wait()
+
+        def body(r):
+            value = up[r, :].astype(jnp.bfloat16)
+            low[r, :] = value
+            gather_row(3 * layers + l, value.astype(jnp.float32))
+        each_tile(m, body)
+        fill(lambda r, c: dot_tn(hidden[:m, r], low[:m, c]))
+        if saved[l][0].dtype == jnp.bfloat16:
+            load(l, "current").start()
+        else:
+            next_load(l, "hidden")
+
+    def expand(l):
+        m = count(l)
+        fetch(l * UNITS + 5).wait()
+        load(l, "pre").wait()
+
+        def body(r):
+            grown = dot_nt(low[r, :], weight[...])
+            value = wide_a[r, :]
+            gate = 1.0 / (1.0 + jnp.exp(-value))
+            result = (grown * gate * (1.0 + value * (1.0 - gate))).astype(jnp.bfloat16)
+            pre_low[r, :] = result
+            gather_row(2 * layers + l, result.astype(jnp.float32))
+        each_tile(m, body)
+        fetch(l * UNITS + 4).start()
+        load(l, "mixed").wait()
+        fill(lambda r, c: dot_tn(mixed[:m, r], pre_low[:m, c]))
+        next_load(l, "mixed")
+
+    def output(l):
+        m = count(l)
+        fetch(l * UNITS + 4).wait()
+        load(l, "after").wait()
+        gain = vector(2 * l + 1)
+
+        def body(r):
+            w = dot_nt(pre_low[r, :], weight[...])
+            value = up[r, :] + norm_tile(wide_b[r, :], gain, w, 2 * l + 1)
+            up[r, :] = value
+            low[r, :] = value.astype(jnp.bfloat16)
+        each_tile(m, body)
+        fetch(l * UNITS + 3).start()
+        if saved[l][0].dtype != jnp.bfloat16:
+            load(l, "current").start()
+        load(l, "att").wait()
+        fill(lambda r, c: dot_nn(att[r, :m], low[:m, c]))
+        load(l, "normed_t").start()
+
+    def attention(l):
+        m = count(l)
+        fetch(l * UNITS + 3).wait()
+
+        def body(r):
+            do[r, :m] = dot_nt(weight[r, :], low[:m, :]).astype(jnp.bfloat16)
+        each_tile(width, body)
+        fetch(l * UNITS + 1).start()
+        for name in ("q", "k", "v", "lse"):
+            load(l, name).wait()
+        row = 4 * layers + l
+        factor = jnp.broadcast_to(vec[row : row + 1, 0:128], (128, 128)).T[0:HEAD, 0:1]
+
+        def head(h, sums):
+            rows = head_rows(h)
+            kh, vh, qh, oh = k[rows, :], v[rows, :], q[rows, :m], do[rows, :m]
+            scores = dot_tn(kh, qh) + bias_ref[:, :m]
+            probs = jnp.exp(scores - lse[h, :, :m])
+            weighted = probs * dot_tn(vh, oh)
+            inner = jnp.sum(weighted, axis=0, keepdims=True)
+            score = (weighted - probs * inner).astype(jnp.bfloat16)
+            v[rows, :] = dot_nt(oh, probs.astype(jnp.bfloat16)).astype(jnp.bfloat16)
+            k[rows, :] = dot_nt(qh, score).astype(jnp.bfloat16)
+            query = dot_nn(kh, score)
+            q[rows, :m] = (query * factor).astype(jnp.bfloat16)
+            return sums + jnp.sum(query * qh.astype(jnp.float32), axis=1, keepdims=True)
+
+        sums = lax.fori_loop(0, HEADS, head, jnp.zeros((HEAD, 1), jnp.float32))
+        flat = jnp.broadcast_to(sums, (HEAD, 128)).T
+        tiny[row : row + 1, 0:HEAD] = flat[0:1, :]
+        next_load(l, "lse")
+
+    def project(l, n):
+        source = (k, v, q)[n]
+        m = total if n < 2 else count(l)
+        if n == 0:
+            attention(l)
+            load(l, "normed_t").wait()
+        fill(lambda r, c: dot_nt(att[r, :m], source[c, :m]))
+        fetch(l * UNITS + (1, 2, 0)[n]).wait()
+        if n == 2:
+            load(l, "current").wait()
+        gain = vector(2 * l)
+        current = hidden if saved[l][0].dtype == jnp.bfloat16 else wide_b
+
+        def body(r):
+            value = dot_nt(source[:, r].T, weight[...])
+            if n > 0:
+                value = value + wide_a[r, :]
+            wide_a[r, :] = value
+        each_tile(m, body)
+        if n < 2:
+            fetch(l * UNITS + (2, 0)[n]).start()
+            return
+        if l > 0:
+            fetch((l - 1) * UNITS + 5).start()
+
+        def close(r):
+            return norm_tile(current[r, :].astype(jnp.float32), gain, wide_a[r, :], 2 * l)
+
+        own = count(l)
+
+        def first(r):
+            up[r, :] = up[r, :] + close(r)
+        each_tile(own, first)
+        if own < total:
+            @pl.loop(own // ROWS, total // ROWS)
+            def _(i):
+                r = pl.ds(pl.multiple_of(i * ROWS, ROWS), ROWS)
+                up[r, :] = close(r)
+        next_load(l, "pre", "after", "att", "q", "k", "v")
+        if l == 0:
+            sent[...] = up[length:, :].astype(jnp.bfloat16)
+            reply.start()
+
+    reply = remote(sent, came, x_sem.at[0], x_sem.at[1], at.x())
+    work = (
+        down, expand, output,
+        lambda l: project(l, 0), lambda l: project(l, 1), lambda l: project(l, 2),
+    )
+    last = layers - 1
+    start_copy = pltpu.make_async_copy(cot_ref, sent, x_sem.at[2])
+    start_copy.start()
+    for name in ("hidden", "pre", "mixed", "after", "att", "q", "k", "v", "lse"):
+        load(last, name).start()
+    fetch(last * UNITS + 5).start()
+    tiny[...] = jnp.zeros_like(tiny)
+    at.greet()
+    start_copy.wait()
+    up[:length, :] = sent[...].astype(jnp.float32)
+
+    @pl.loop(0, reduce.iterations)
+    def _(i):
+        for n in range(units):
+            @pl.when(i == n)
+            def _(n=n):
+                work[n % UNITS](last - n // UNITS)
+        reduce.step(i)
+        for n in range(5):
+            @pl.when(i == units + n)
+            def _(n=n):
+                reduce.tiny_step(n)
+                if n == 2:
+                    reply.wait()
+                    input_ref[...] = (up[:length, :] + came[...].astype(jnp.float32)).astype(jnp.bfloat16)
+
+
+def backward_pass(nz, cotangent, full, vec, bias, saved):
+    layers = len(saved)
+    units = layers * UNITS
+    length, width = cotangent.shape
+    total = bias.shape[0]
+    shard = width // (2 * nz)
+    half, wide, low, n = shard // 2, width // 2, nz // 2, nz - 1
+    slots = min(5, units)
+    flat = [one for group in saved for one in group]
+    rows = vec.shape[0]
+    dma = pltpu.SemaphoreType.DMA
+    small, large = jnp.bfloat16, jnp.float32
+    anywhere = pl.BlockSpec(memory_space=pl.ANY)
+    inside = pl.BlockSpec(memory_space=pltpu.VMEM)
+    natural, turned = (total, width), (width, total)
+    return pl.pallas_call(
+        functools.partial(backward_kernel, nz, layers, length, total),
+        out_shape=(
+            jax.ShapeDtypeStruct((units, shard, width), small),
+            jax.ShapeDtypeStruct((rows, width), large),
+            jax.ShapeDtypeStruct((length, width), small),
+        ),
+        in_specs=[anywhere, anywhere, inside, inside] + [anywhere] * len(flat),
+        out_specs=(anywhere, inside, inside),
+        scratch_shapes=[
+            pltpu.VMEM(natural, large),
+            pltpu.VMEM(natural, large),
+            pltpu.VMEM(natural, large),
+            pltpu.VMEM(natural, small),
+            pltpu.VMEM(natural, small),
+            pltpu.VMEM(natural, small),
+            pltpu.VMEM(natural, small),
+            pltpu.VMEM(turned, small),
+            pltpu.VMEM(turned, small),
+            pltpu.VMEM(turned, small),
+            pltpu.VMEM(turned, small),
+            pltpu.VMEM(turned, small),
+            pltpu.VMEM((HEADS, 1, total), large),
+            pltpu.VMEM((width, width), small),
+            pltpu.VMEM((length, width), small),
+            pltpu.VMEM((length, width), small),
+            dma((layers, 11)),
+            dma((1,)),
+            dma((3,)),
+            pltpu.VMEM((rows, width), large),
+            pltpu.VMEM((nz, 2, shard, width), small),
+            pltpu.VMEM((slots, nz, shard, width), small),
+            pltpu.VMEM((units, low, shard, wide), small),
+            pltpu.VMEM((units, low, half, width), small),
+            pltpu.VMEM((units, low, half, wide), small),
+            pltpu.VMEM((units, low, half, wide), small),
+            pltpu.VMEM((units, n, half, wide), small),
+            pltpu.VMEM((units, half, wide), small),
+            pltpu.VMEM((3 + n, rows, width), large),
+            dma((units,)), dma((units,)),
+            dma((units, 2)), dma((units, 2)),
+            dma((units, 2)), dma((units, 2)),
+            dma((units, n)), dma((units, n)),
+            dma((units,)),
+            dma((units, 4)), dma((units, 4)),
+            dma((3 + n,)), dma((3 + n,)),
+            pltpu.SemaphoreType.REGULAR,
+        ],
+        compiler_params=pltpu.CompilerParams(
+            collective_id=2, has_side_effects=True, vmem_limit_bytes=63 << 20
+        ),
+    )(cotangent, full, vec, bias, *flat)
+
+
 def forward_layer(current, weights, allowed, series_count, local_length, total_length):
     qkv_weight, out_weight, up_weight, down_weight, norm_gains, up_bias, down_bias, query_scale = (
         weights
@@ -60,8 +1156,8 @@
     normed, inverse_one = norm_rows(current, norm_gains[0].astype(jnp.float32))
     normed_low = normed.astype(jnp.bfloat16).reshape(series_count, local_length, model_width)
     projected = jnp.einsum(
-        "bld,dc->bcl", normed_low, qkv_weight, preferred_element_type=jnp.float32
-    )
+        "bld,kdc->bkcl", normed_low, qkv_weight, preferred_element_type=jnp.float32
+    ).reshape(series_count, 3 * model_width, local_length)
     query_raw = projected[:, :model_width]
     factor = query_factor(query_scale)
     query_low = (
@@ -180,20 +1276,15 @@
     query_grad = jnp.einsum(
         "bhqk,bhek->bheq", score_low, key_all, preferred_element_type=jnp.float32
     )
-    key_local, value_local = (
-        lax.psum_scatter(
+    pair_grad = jnp.concatenate(
+        [
             key_grad.reshape(series_count, model_width, total_length),
-            "seq",
-            scatter_dimension=2,
-            tiled=True,
-        ),
-        lax.psum_scatter(
             value_grad.reshape(series_count, model_width, total_length),
-            "seq",
-            scatter_dimension=2,
-            tiled=True,
-        ),
-    )
+        ],
+        axis=1,
+    )
+    pair_local = lax.psum_scatter(pair_grad, "seq", scatter_dimension=2, tiled=True)
+    key_local, value_local = pair_local[:, :model_width], pair_local[:, model_width:]
     factor = query_factor(query_scale)
     factor_grad = jnp.sum(
         query_grad * query_raw.reshape(series_count, HEADS, HEAD, local_length), axis=(0, 1, 3)
@@ -213,7 +1304,10 @@
         "bld,bcl->dc", normed_low, projected_grad, preferred_element_type=jnp.float32
     )
     normed_grad = jnp.einsum(
-        "bcl,dc->bld", projected_grad, qkv_weight, preferred_element_type=jnp.float32
+        "bkcl,kdc->bld",
+        projected_grad.reshape(series_count, 3, model_width, local_length),
+        qkv_weight,
+        preferred_element_type=jnp.float32,
     ).reshape(token_count, model_width)
     norm_grad_one, gain_grad_one = norm_back(
         current, inverse_one, norm_gains[0].astype(jnp.float32), normed_grad
@@ -232,7 +1326,60 @@
     return (result, layer_grads)
 
 
-def shards(
+def pack_small(norm_gains, up_bias, down_bias, query_scale):
+    layers, _, shard = norm_gains.shape
+    scale = jnp.pad(query_scale, ((0, 0), (0, shard - query_scale.shape[1])))
+    rows = jnp.concatenate([norm_gains.reshape(2 * layers, shard), up_bias, down_bias, scale])
+    return jnp.pad(rows, ((0, -rows.shape[0] % 16), (0, -shard % 128)))
+
+
+def unpack_small(tiny, layers, shard, scale_shard):
+    count = tiny.shape[0]
+    vectors = tiny[:, : 4 * layers, :shard].transpose(1, 0, 2).reshape(4 * layers, count * shard)
+    scale = tiny[:, 4 * layers : 5 * layers, :scale_shard].transpose(1, 0, 2).reshape(layers, count * scale_shard)
+    gains = vectors[: 2 * layers].reshape(layers, 2, count * shard)
+    return gains, vectors[2 * layers : 3 * layers], vectors[3 * layers :], scale
+
+
+def pack_tiny(layer_grads, count):
+    gains = jnp.concatenate([g[4] for g in layer_grads])
+    vectors = jnp.concatenate(
+        [gains, jnp.stack([g[5] for g in layer_grads]), jnp.stack([g[6] for g in layer_grads])]
+    )
+    scale = jnp.stack([g[7] for g in layer_grads])
+    shard, part = vectors.shape[1] // count, scale.shape[1] // count
+    vectors = vectors.reshape(-1, count, shard)
+    scale = jnp.pad(scale.reshape(-1, count, part), ((0, 0), (0, 0), (0, shard - part)))
+    rows = jnp.concatenate([vectors, scale]).transpose(1, 0, 2)
+    return jnp.pad(rows, ((0, 0), (0, -rows.shape[1] % 16), (0, -shard % 128)))
+
+
+def unpack_tiny(tiny, layers, shard, part):
+    gains = tiny[: 2 * layers, :shard].reshape(layers, 2, shard)
+    up, down = tiny[2 * layers : 3 * layers, :shard], tiny[3 * layers : 4 * layers, :shard]
+    return gains, up, down, tiny[4 * layers : 5 * layers, :part]
+
+
+def gather_plain(qkv_weight, out_weight, up_weight, down_weight, small):
+    layers, shard, width = out_weight.shape
+    qkv = qkv_weight.reshape(layers, shard, 3, width).transpose(0, 2, 1, 3)
+    square = jnp.stack([out_weight, up_weight, down_weight], axis=1)
+    units = jnp.concatenate([qkv, square], axis=1).reshape(layers * UNITS, shard, width)
+    full = lax.all_gather(units, "fsdp", axis=1, tiled=True)
+    return full, lax.all_gather(small, "fsdp", axis=0)
+
+
+def reduce_plain(layer_grads, tiny):
+    units = []
+    for grads in layer_grads:
+        width = grads[0].shape[1]
+        units += list(grads[:3]) + [grads[3][:, k * width : (k + 1) * width] for k in range(3)]
+    shares = lax.psum_scatter(jnp.stack(units), "fsdp", scatter_dimension=1, tiled=True)
+    small = lax.psum_scatter(tiny, "fsdp", scatter_dimension=0, tiled=True)[0]
+    return lax.psum(shares, ("replica", "seq")), lax.psum(small, ("replica", "seq"))
+
+
+def plain(
     series_in,
     cotangent,
     qkv_weight,
@@ -249,106 +1396,126 @@
 ):
     series_count, local_length, model_width = series_in.shape
     seq_count = lax.axis_size("seq")
+    group = lax.axis_size("fsdp")
     total_length = local_length * seq_count
     offset = lax.axis_index("seq") * local_length
     allowed = visible(pad_length, span_starts, span_count, offset, local_length, total_length)
-    layer_count = qkv_weight.shape[0]
+    layer_count, shard = qkv_weight.shape[:2]
+    scale_shard = query_scale.shape[1]
+    small = pack_small(norm_gains, up_bias, down_bias, query_scale)
+    full, tiny = gather_plain(qkv_weight, out_weight, up_weight, down_weight, small)
+    gains, up_full, down_full, scale_full = unpack_small(tiny, layer_count, shard, scale_shard)
+    weights = [
+        (
+            full[UNITS * l : UNITS * l + 3],
+            full[UNITS * l + 3],
+            full[UNITS * l + 4],
+            full[UNITS * l + 5],
+            gains[l],
+            up_full[l],
+            down_full[l],
+            scale_full[l],
+        )
+        for l in range(layer_count)
+    ]
     current = series_in.reshape(series_count * local_length, model_width).astype(jnp.float32)
-    gathered_list = []
     stored_list = []
-    for layer_index in range(layer_count):
-        gathered = (
-            lax.all_gather(qkv_weight[layer_index], "fsdp", axis=0, tiled=True),
-            lax.all_gather(out_weight[layer_index], "fsdp", axis=0, tiled=True),
-            lax.all_gather(up_weight[layer_index], "fsdp", axis=0, tiled=True),
-            lax.all_gather(down_weight[layer_index], "fsdp", axis=0, tiled=True),
-            lax.all_gather(norm_gains[layer_index], "fsdp", axis=1, tiled=True),
-            lax.all_gather(up_bias[layer_index], "fsdp", axis=0, tiled=True),
-            lax.all_gather(down_bias[layer_index], "fsdp", axis=0, tiled=True),
-            lax.all_gather(query_scale[layer_index], "fsdp", axis=0, tiled=True),
+    for l in range(layer_count):
+        current, stored = forward_layer(
+            current, weights[l], allowed, series_count, local_length, total_length
         )
-        current, stored = forward_layer(
-            current, gathered, allowed, series_count, local_length, total_length
-        )
-        gathered_list.append(gathered)
         stored_list.append(stored)
     series_out = current.reshape(series_count, local_length, model_width).astype(jnp.bfloat16)
     upstream = cotangent.reshape(series_count * local_length, model_width).astype(jnp.float32)
-    owned_list = [None] * layer_count
-    for layer_index in reversed(range(layer_count)):
-        gathered = (
-            lax.all_gather(qkv_weight[layer_index], "fsdp", axis=0, tiled=True),
-            lax.all_gather(out_weight[layer_index], "fsdp", axis=0, tiled=True),
-            lax.all_gather(up_weight[layer_index], "fsdp", axis=0, tiled=True),
-            lax.all_gather(down_weight[layer_index], "fsdp", axis=0, tiled=True),
-            lax.all_gather(norm_gains[layer_index], "fsdp", axis=1, tiled=True),
-            lax.all_gather(up_bias[layer_index], "fsdp", axis=0, tiled=True),
-            lax.all_gather(down_bias[layer_index], "fsdp", axis=0, tiled=True),
-            lax.all_gather(query_scale[layer_index], "fsdp", axis=0, tiled=True),
+    order = list(reversed(range(layer_count)))
+    grads_list = {}
+    for l in order:
+        upstream, grads_list[l] = backward_layer(
+            upstream, weights[l], stored_list[l], allowed, series_count, local_length, total_length
         )
-        upstream, layer_grads = backward_layer(
-            upstream,
-            gathered,
-            stored_list[layer_index],
-            allowed,
-            series_count,
-            local_length,
-            total_length,
-        )
-        shares = (
-            lax.psum_scatter(
-                layer_grads[0].astype(jnp.bfloat16), "fsdp", scatter_dimension=0, tiled=True
-            ).astype(jnp.float32),
-            lax.psum_scatter(
-                layer_grads[1].astype(jnp.bfloat16), "fsdp", scatter_dimension=0, tiled=True
-            ).astype(jnp.float32),
-            lax.psum_scatter(
-                layer_grads[2].astype(jnp.bfloat16), "fsdp", scatter_dimension=0, tiled=True
-            ).astype(jnp.float32),
-            lax.psum_scatter(
-                layer_grads[3].astype(jnp.bfloat16), "fsdp", scatter_dimension=0, tiled=True
-            ).astype(jnp.float32),
-            lax.psum_scatter(
-                layer_grads[4].astype(jnp.bfloat16), "fsdp", scatter_dimension=1, tiled=True
-            ).astype(jnp.float32),
-            lax.psum_scatter(
-                layer_grads[5].astype(jnp.bfloat16), "fsdp", scatter_dimension=0, tiled=True
-            ).astype(jnp.float32),
-            lax.psum_scatter(
-                layer_grads[6].astype(jnp.bfloat16), "fsdp", scatter_dimension=0, tiled=True
-            ).astype(jnp.float32),
-            lax.psum_scatter(
-                layer_grads[7].astype(jnp.bfloat16), "fsdp", scatter_dimension=0, tiled=True
-            ).astype(jnp.float32),
-        )
-        shares = (
-            lax.psum(shares[0].astype(jnp.bfloat16), ("replica", "seq")).astype(jnp.float32),
-            lax.psum(shares[1].astype(jnp.bfloat16), ("replica", "seq")).astype(jnp.float32),
-            lax.psum(shares[2].astype(jnp.bfloat16), ("replica", "seq")).astype(jnp.float32),
-            lax.psum(shares[3].astype(jnp.bfloat16), ("replica", "seq")).astype(jnp.float32),
-            lax.psum(shares[4].astype(jnp.bfloat16), ("replica", "seq")).astype(jnp.float32),
-            lax.psum(shares[5].astype(jnp.bfloat16), ("replica", "seq")).astype(jnp.float32),
-            lax.psum(shares[6].astype(jnp.bfloat16), ("replica", "seq")).astype(jnp.float32),
-            lax.psum(shares[7].astype(jnp.bfloat16), ("replica", "seq")).astype(jnp.float32),
-        )
-        owned_list[layer_index] = shares
-    stacked = [
-        jnp.stack([owned_list[layer_index][member_index] for layer_index in range(layer_count)])
-        for member_index in range(8)
+    tiny_grads = pack_tiny([grads_list[l] for l in range(layer_count)], group)
+    big = [
+        tuple(grads_list[l][k].astype(jnp.bfloat16) for k in (3, 2, 1, 0)) for l in order
     ]
+    shares, tiny_sum = reduce_plain(big, tiny_grads)
+    shares = shares.reshape(layer_count, UNITS, shard, model_width)[::-1]
+    grad_gains, grad_up_bias, grad_down_bias, grad_scale = unpack_tiny(
+        tiny_sum, layer_count, shard, scale_shard
+    )
+    grad_qkv = shares[:, 3:].transpose(0, 2, 1, 3).reshape(layer_count, shard, 3 * model_width)
     input_grad = upstream.reshape(series_count, local_length, model_width).astype(jnp.bfloat16)
     return (
         series_out,
         input_grad,
-        stacked[0],
-        stacked[1],
-        stacked[2],
-        stacked[3],
-        stacked[4],
-        stacked[5],
-        stacked[6],
-        stacked[7],
-    )
+        grad_qkv.astype(jnp.float32),
+        shares[:, 2].astype(jnp.float32),
+        shares[:, 1].astype(jnp.float32),
+        shares[:, 0].astype(jnp.float32),
+        grad_gains,
+        grad_up_bias,
+        grad_down_bias,
+        grad_scale,
+    )
+
+
+def finish(shares, tiny, layers, shard, width, query_scale):
+    shares = shares.reshape(layers, UNITS, shard, width)[::-1]
+    low = jnp.float32
+    place = lax.axis_index("fsdp")
+    part = query_scale.shape[1]
+    vectors = lax.dynamic_slice_in_dim(tiny[: 4 * layers], place * shard, shard, axis=1)
+    scale = lax.dynamic_slice_in_dim(tiny[4 * layers : 5 * layers], place * part, part, axis=1)
+    raw = query_scale.astype(jnp.float32)
+    scale = scale * (jax.nn.sigmoid(raw) * (SOFT_ONE / math.sqrt(HEAD))) / query_factor(query_scale)
+    qkv = jnp.concatenate([shares[:, 5], shares[:, 3], shares[:, 4]], axis=2)
+    return (
+        qkv.astype(low),
+        shares[:, 2].astype(low),
+        shares[:, 1].astype(low),
+        shares[:, 0].astype(low),
+        vectors[: 2 * layers].reshape(layers, 2, shard),
+        vectors[2 * layers : 3 * layers],
+        vectors[3 * layers :],
+        scale,
+    )
+
+
+def fused(
+    series_in,
+    cotangent,
+    qkv_weight,
+    out_weight,
+    up_weight,
+    down_weight,
+    norm_gains,
+    up_bias,
+    down_bias,
+    query_scale,
+    pad_length,
+    span_starts,
+    span_count,
+):
+    length = series_in.shape[1]
+    layers, shard, width = out_weight.shape
+    nz = lax.axis_size("fsdp") // 2
+    small = pack_small(norm_gains, up_bias, down_bias, query_scale)
+    bias = pair_bias(pad_length, span_starts, span_count, length)
+    full, vec, series_out, saved = forward_pass(
+        nz, series_in[0], qkv_weight, out_weight, up_weight, down_weight, small, bias, query_scale.shape[1]
+    )
+    shares, tiny, input_grad = backward_pass(nz, cotangent[0], full, vec, bias, saved)
+    rest = finish(shares, tiny, layers, shard, width, query_scale)
+    return (series_out[None], input_grad[None]) + rest
+
+
+def shards(*args):
+    series_in, out_weight = args[0], args[3]
+    group = lax.axis_size("fsdp")
+    width = series_in.shape[2]
+    block = lax.axis_size("replica") == 2 and lax.axis_size("seq") == 2 and group % 4 == 0
+    block = block and series_in.shape[0] == 1 and width == out_weight.shape[2] == HEADS * HEAD
+    block = block and (width // group) % 32 == 0 and width % 256 == 0
+    return fused(*args) if block else plain(*args)
 
 
 def solution(mesh):

time: 1420 us -> 490 us (0.35)
  waiting for transfers between devices: 971 us -> 0 us
  Pallas kernels: 0 us -> 464 us
  matrix products: 173 us -> 0 us
  blocking collectives: 96.6 us -> 0 us
  other arithmetic: 82.8 us -> 12 us
  local copies, waits for them, and re-layouts: 59.5 us -> 8.61 us
  between operations: 21.9 us -> 4.62 us
    reduce_scatter x12 -> x0, waiting for transfers between devices: 520 us -> none  [the longest x2 208 us: shards(): lax.psum_scatter(layer_grads[0].astype(jnp.bfloat16), 'fsdp', scatter_dim...]
    pallas_call x0 -> x2, Pallas kernels: none -> 464 us  [the longest x1 287 us: backward_pass(): pl.pallas_call(functools.partial(backward_kernel, nz, layers, length, tot...]
    all_gather x10 -> x0, waiting for transfers between devices: 313 us -> none  [the longest x2 148 us: shards(): lax.all_gather(qkv_weight[layer_index], 'fsdp', axis=0, tiled=True)]
    dot_general x36 -> x0, matrix products: 173 us -> none  [the longest x2 19.5 us: forward_layer(): jnp.einsum('bhqk,bhek->bheq', probs_low, value_all, preferred_element_typ...]
    psum x1 -> x0, waiting for transfers between devices: 108 us -> none  [shards(): lax.psum(shares[0].astype(jnp.bfloat16), ('replica', 'seq'))]
    unnamed x2 -> x0, blocking collectives: 52.9 us -> none
    mul x7 -> x0, other arithmetic: 42.5 us -> none  [the longest x2 41.9 us: norm_rows(): return (values * inverse * scale_gain, inverse)]
    all_gather x2 -> x0, blocking collectives: 33.7 us -> none  [shards(): lax.all_gather(norm_gains[layer_index], 'fsdp', axis=1, tiled=True)]
  transfers between devices with their start and end apart: 25 -> 0, of which waited for: 21 -> 0; matrix products, arithmetic and copies ran while one was open for 16% -> 0% of each run, Pallas kernels for 0% -> 0%
where the time goes in v1:
time: 490 us; the launch traced here: 489 us
  Pallas kernels  464 us (95%)
  other arithmetic  12 us (2%)
  local copies, waits for them, and re-layouts  8.61 us (2%)
    pallas_call x1, Pallas kernels, backward_pass(): pl.pallas_call(functools.partial(backward_kernel, nz, layers, length, tot...  287 us
    pallas_call x1, Pallas kernels, forward_pass(): pl.pallas_call(functools.partial(forward_kernel, nz, layers, part), out_s...  177 us

profile of v1, /device:TPU:0, one launch (start us, length us, event | category | flops | bytes accessed | tf_op | source)
XLA Modules:
  0.0 489.3 jit_solution(14446929571632305642)
XLA Ops:
  0.6 0.7 reshape.237
  1.3 0.7 fusion.1
  2.1 0.6 pad.9.refs_5_
  2.7 1.4 fusion.14
  7.3 2.0 and_and_fusion.3
  9.9 0.7 and_and_fusion.2
  10.6 1.6 or_select_fusion.refs_6_.refs_3_
  12.2 177.0 %shard_map.204 = (bf16[12,1280,1280]{2,1,0:T(8,128)(2,1)}, f32[16,1280]{1,0:T(8,128)}, bf16[256,1280]{1,0:T(8,128)(2,1)}, bf16[512,1280]{1,0:T(8,128)(2,1)}, bf1...) custom-call(bf16[256,1280]{1,0:T(8,128)(2,1)} %bitcast.44, ...), custom_call_target="tpu_custom_call" | custom-call | tf_op jit(solution)/shard_map/pallas_call | solution.py:602
  189.2 287.1 %shard_map.205 = (bf16[12,160,1280]{2,1,0:T(8,128)(2,1)}, f32[16,1280]{1,0:T(8,128)}, bf16[256,1280]{1,0:T(8,128)(2,1)}) custom-call(bf16[256,1280]{1,0:T(8,128)(2,1)} %bitcast.43, bf16[12,1280,1280]{2,1,0:T(8,128)(2,1)} %get-tuple-element.39.refs_1_, f32[16,1280]{1,0:T(8,128)} %get-tuple-element.40.refs_2_, f32[512,512]{1,0:T(8,128)} %or_select_fusion.refs_6_.refs_3_, ...), custom_call_target="tpu_custom_call" | custom-call | tf_op jit(solution)/shard_map/pallas_call | solution.py:1097
  476.3 2.7 slice_bitcast_fusion
  479.0 0.1 reverse_bitcast_fusion
  479.1 0.1 reverse_bitcast_fusion.1
  479.1 0.1 reverse_bitcast_fusion.2
  479.2 2.6 maximum_convert_fusion
  481.8 1.3 bitcast_convert_fusion.2
  483.1 1.3 bitcast_convert_fusion.1
  484.3 0.0 copy-start.2
  484.3 0.0 copy-start.3
  484.3 0.0 copy-start
  484.3 0.0 copy-start.1
  484.3 1.3 bitcast_convert_fusion
  485.6 0.0 copy-done.2
  485.6 0.1 constant_dynamic-slice_fusion
  485.7 0.6 reshape.239
  486.3 0.7 fusion.13
  487.0 0.0 copy-done.3
  487.0 0.6 fusion.7
  487.6 0.0 copy-done
  487.6 0.8 copy.39
  488.4 0.0 copy-done.1
  488.4 0.8 copy.40
  (4 shorter events, 0.0 us)
Async XLA Ops:
  484.3 1.3 copy-start.2
  484.3 2.6 copy-start.3
  484.3 3.3 copy-start
  484.3 4.1 copy-start.1
